TPU v7x, 256 devices: a whole 4x4x8 slice. The times are simulated.
256 devices in a mesh: px: 16 (over y, x), py: 16 (over z, core).
Axes of the slice: x: 4, y: 4, z: 8, core: 2. Of those that a mesh axis runs over, the one named last changes fastest.
Arguments:
- start_field: float32 [128, 256, 512], P('px', 'py'), may hold values from -1.7 to 1.7
- known: float32 [8, 128, 256, 512], P(None, 'px', 'py'), may hold values from -1 to 1
Outputs:
- solution_field: float32 [128, 256, 512], P('px', 'py')
- residual: float32 [128, 256, 512], P('px', 'py')
All inputs are finite; a program needn't handle non-finite values.
Results may differ from a plain program's by a relative error of at most 0.01.
Values sent between devices are 32-bit elements; how exact they have to be, the bound alone decides.
No kernel may reach another device: no remote copies, remote signals or barrier semaphores. Data moves between devices by JAX's collectives and lax.ppermute only.
A program may use at most 64 MiB of HBM per device.

v0:
```python
import jax
import jax.numpy as jnp
from jax import lax
from jax.sharding import PartitionSpec as P

NEWTON = 2
ITERS = 3


DIFFUSION = 0.5
SHIFT = 4.0
EPS = 1e-06


def extended(cells, sides, width):
    for axis, dim in sides:
        count = lax.axis_size(axis)
        ends = count - 1
        head = lax.slice_in_dim(cells, 0, width, axis=dim)
        tail = lax.slice_in_dim(cells, cells.shape[dim] - width, cells.shape[dim], axis=dim)
        cells = jnp.concatenate(
            [
                lax.ppermute(tail, axis, [(i, (i + 1) % count) for i in range(ends)]),
                cells,
                lax.ppermute(head, axis, [((i + 1) % count, i) for i in range(ends)]),
            ],
            axis=dim,
        )
    return cells


def laplace(field):
    padded = extended(field, (("px", 0), ("py", 1)), 1)
    zero = jnp.zeros_like(field[:, :, :1])
    upper = jnp.concatenate([field[:, :, 1:], zero], axis=2)
    lower = jnp.concatenate([zero, field[:, :, :-1]], axis=2)
    beside = padded[2:, 1:-1, :] + padded[:-2, 1:-1, :]
    beside = beside + padded[1:-1, 2:, :] + padded[1:-1, :-2, :]
    return beside + upper + lower - 6.0 * field


def allen_cahn(field, lap):
    return DIFFUSION * lap + field - field * field * field


def solve_small(hess, beta):
    normal = jnp.sum(hess[:, :, None] * hess[:, None, :], axis=0)
    target = beta * hess[0]
    lower = jnp.linalg.cholesky(normal)
    count = normal.shape[0]
    forward = []
    for i in range(count):
        acc = target[i]
        for j in range(i):
            acc = acc - lower[i, j] * forward[j]
        forward.append(acc / lower[i, i])
    back = [None] * count
    for i in reversed(range(count)):
        acc = forward[i]
        for j in range(i + 1, count):
            acc = acc - lower[j, i] * back[j]
        back[i] = acc / lower[i, i]
    return jnp.stack(back)


def local(start_field, known):
    cells = float(
        start_field.shape[0]
        * lax.axis_size("px")
        * start_field.shape[1]
        * lax.axis_size("py")
        * start_field.shape[2]
    )
    field = start_field
    lap_field = laplace(field)
    for step in range(NEWTON):
        force = allen_cahn(field, lap_field)
        diffs = field[None] - known
        dist_local = jnp.sum(diffs * diffs, axis=(1, 2, 3))
        first_sum, force_sq = lax.psum((dist_local, jnp.sum(force * force)), ("px", "py"))
        beta = jnp.sqrt(force_sq + EPS)
        basis = [-force / beta]
        lap_basis = []
        jac_diag = 1.0 - 3.0 * field * field
        hess = jnp.zeros((ITERS + 1, ITERS), jnp.float32)
        for k in range(ITERS):
            lap_vec = laplace(basis[k])
            lap_basis.append(lap_vec)
            image = DIFFUSION * lap_vec + jac_diag * basis[k]
            heights_local = jnp.stack([jnp.sum(vec * image) for vec in basis])
            summed = lax.psum(heights_local, ("px", "py"))
            rest = image
            for j in range(k + 1):
                rest = rest - summed[j] * basis[j]
            height = jnp.sqrt(lax.psum(jnp.sum(rest * rest), ("px", "py")) + EPS)
            hess = hess.at[: k + 1, k].set(summed).at[k + 1, k].set(height)
            if k < ITERS - 1:
                basis.append(rest / height)
        coeffs = solve_small(hess, beta)
        delta = coeffs[0] * basis[0]
        for j in range(1, ITERS):
            delta = delta + coeffs[j] * basis[j]
        inner = lax.psum(jnp.sum(diffs * delta[None], axis=(1, 2, 3)), ("px", "py"))
        mean_dist = first_sum / cells + EPS
        weight = 1.0 / mean_dist + SHIFT
        total = jnp.sum(2.0 * inner / (cells * mean_dist * mean_dist * weight))
        scale = 1.0 / (1.0 + jnp.abs(total))
        field = field + scale * delta
        lap_field = laplace(field)
    return (field, allen_cahn(field, lap_field))


def solution(mesh):
    placed = (P("px", "py", None), P(None, "px", "py", None))
    return jax.shard_map(
        local,
        mesh=mesh,
        in_specs=placed,
        out_specs=(P("px", "py", None), P("px", "py", None)),
        check_vma=False,
    )
```

profile of v0, /device:TPU:1, one launch (start us, length us, event | category | flops | bytes accessed | tf_op | source)
XLA Modules:
  0.0 1434.4 jit_solution(6165251050151356504)
XLA Ops:
  2.8 4.6 collective-permute-start.1
  9.6 5.5 collective-permute-start.2
  15.1 1.9 collective-permute-start.3
  19.1 83.2 %psum.126 = f32[]{:T(128)} all-reduce(f32[]{:T(128)} %get-tuple-element.179), channel_id=1, replica_groups=mesh['px'=16,'py'=16] {'px','py'}, use_global_device_ids=true, to_apply=%region_1.0 | all-reduce | flops 1 | bytes 8 | tf_op jit(solution)/shard_map/psum | solution.py:80
  103.1 2.4 collective-permute-start.5
  107.5 2.7 collective-permute-done.4
  110.2 4.0 collective-permute-start.6
  114.2 2.6 collective-permute-start.7
  118.5 77.3 %psum.127 = f32[1]{0:T(128)} all-reduce(f32[1]{0:T(128)} %bitcast), channel_id=1, replica_groups=mesh['px'=16,'py'=16] {'px','py'}, use_global_device_ids=true, to_apply=%region_3.0 | all-reduce | flops 1 | bytes 8 | tf_op jit(solution)/shard_map/psum | solution.py:91
  197.1 74.0 %psum.128 = f32[]{:T(128)} all-reduce(f32[]{:T(128)} %multiply_reduce_fusion.21), channel_id=1, replica_groups=mesh['px'=16,'py'=16] {'px','py'}, use_global_device_ids=true, to_apply=%region_5.0 | all-reduce | flops 1 | bytes 8 | tf_op jit(solution)/shard_map/psum | solution.py:95
  272.5 2.3 collective-permute-start.9
  277.4 2.1 collective-permute-done.8
  279.6 4.0 collective-permute-start.10
  283.6 2.8 collective-permute-start.11
  289.7 76.7 %psum.129 = f32[2]{0:T(128)S(1)} all-reduce(f32[2]{0:T(128)S(1)} %pad_maximum_fusion.92), channel_id=1, replica_groups=mesh['px'=16,'py'=16] {'px','py'}, use_global_device_ids=true, to_apply=%region_9.0 | all-reduce | flops 2 | bytes 16 | tf_op jit(solution)/shard_map/psum | solution.py:91
  367.0 2.0 multiply_reduce_fusion.18
  369.1 74.3 %psum.130 = f32[]{:T(128)} all-reduce(f32[]{:T(128)} %get-tuple-element.174), channel_id=1, replica_groups=mesh['px'=16,'py'=16] {'px','py'}, use_global_device_ids=true, to_apply=%region_11.0 | all-reduce | flops 1 | bytes 8 | tf_op jit(solution)/shard_map/psum | solution.py:95
  444.1 2.3 collective-permute-start.13
  448.6 2.5 collective-permute-done.12
  451.1 4.0 collective-permute-start.14
  455.1 2.9 collective-permute-start.15
  458.1 2.0 broadcast_select_fusion.3
  460.1 1.5 scatter.44
  461.6 2.8 multiply_reduce_fusion.17
  464.4 1.9 pad_maximum_fusion.93
  466.5 76.3 %psum.131 = f32[3]{0:T(128)S(1)} all-reduce(f32[3]{0:T(128)S(1)} %pad_maximum_fusion.93), channel_id=1, replica_groups=mesh['px'=16,'py'=16] {'px','py'}, use_global_device_ids=true, to_apply=%region_16.0 | all-reduce | flops 3 | bytes 24 | tf_op jit(solution)/shard_map/psum | solution.py:91
  543.5 1.9 broadcast_select_fusion.1
  545.3 3.6 multiply_reduce_fusion.14
  550.4 73.6 %psum.132 = f32[]{:T(128)} all-reduce(f32[]{:T(128)} %multiply_reduce_fusion.14), channel_id=1, replica_groups=mesh['px'=16,'py'=16] {'px','py'}, use_global_device_ids=true, to_apply=%region_18.0 | all-reduce | flops 1 | bytes 8 | tf_op jit(solution)/shard_map/psum | solution.py:95
  638.0 74.2 %all-reduce.21 = (f32[8]{0:T(128)S(1)}, f32[8]{0:T(128)S(1)}) all-reduce(f32[8]{0:T(128)S(1)} %get-tuple-element.150, f32[8]{0:T(128)S(1)} %get-tuple-element.149), channel_id=1, replica_groups=mesh['px'=16,'py'=16] {'px','py'}, use_global_device_ids=true, to_apply=%region_25.27 | all-reduce | flops 16 | bytes 128 | tf_op jit(solution)/shard_map/psum | solution.py:80
  713.5 3.0 collective-permute-start.17
  717.8 3.3 collective-permute-done.16
  721.2 4.0 collective-permute-start.18
  725.2 2.8 collective-permute-start.19
  729.7 76.5 %psum.135 = f32[]{:T(128)} all-reduce(f32[]{:T(128)} %get-tuple-element.171), channel_id=1, replica_groups=mesh['px'=16,'py'=16] {'px','py'}, use_global_device_ids=true, to_apply=%region_28.0 | all-reduce | flops 1 | bytes 8 | tf_op jit(solution)/shard_map/psum | solution.py:80
  806.9 2.8 collective-permute-start.21
  811.1 3.3 collective-permute-done.20
  814.5 4.0 collective-permute-start.22
  818.5 2.8 collective-permute-start.23
  823.0 77.5 %psum.136 = f32[1]{0:T(128)} all-reduce(f32[1]{0:T(128)} %bitcast.32), channel_id=1, replica_groups=mesh['px'=16,'py'=16] {'px','py'}, use_global_device_ids=true, to_apply=%region_30.0 | all-reduce | flops 1 | bytes 8 | tf_op jit(solution)/shard_map/psum | solution.py:91
  901.8 73.7 %psum.137 = f32[]{:T(128)} all-reduce(f32[]{:T(128)} %multiply_reduce_fusion.11), channel_id=1, replica_groups=mesh['px'=16,'py'=16] {'px','py'}, use_global_device_ids=true, to_apply=%region_32.0 | all-reduce | flops 1 | bytes 8 | tf_op jit(solution)/shard_map/psum | solution.py:95
  976.9 2.3 collective-permute-start.25
  980.5 3.3 collective-permute-done.24
  983.9 4.0 collective-permute-start.26
  987.9 2.8 collective-permute-start.27
  994.0 76.8 %psum.138 = f32[2]{0:T(128)S(1)} all-reduce(f32[2]{0:T(128)S(1)} %pad_maximum_fusion.94), channel_id=1, replica_groups=mesh['px'=16,'py'=16] {'px','py'}, use_global_device_ids=true, to_apply=%region_35.0 | all-reduce | flops 2 | bytes 16 | tf_op jit(solution)/shard_map/psum | solution.py:91
  1071.4 2.0 multiply_reduce_fusion.8
  1073.5 74.2 %psum.139 = f32[]{:T(128)} all-reduce(f32[]{:T(128)} %get-tuple-element.166), channel_id=1, replica_groups=mesh['px'=16,'py'=16] {'px','py'}, use_global_device_ids=true, to_apply=%region_37.0 | all-reduce | flops 1 | bytes 8 | tf_op jit(solution)/shard_map/psum | solution.py:95
  1148.4 2.4 collective-permute-start.29
  1153.0 2.5 collective-permute-done.28
  1156.1 4.0 collective-permute-start.30
  1160.1 2.8 collective-permute-start.31
  1162.9 2.0 broadcast_select_fusion.2
  1166.5 2.7 multiply_reduce_fusion.7
  1169.1 2.0 pad_maximum_fusion.95
  1171.3 76.4 %psum.140 = f32[3]{0:T(128)S(1)} all-reduce(f32[3]{0:T(128)S(1)} %pad_maximum_fusion.95), channel_id=1, replica_groups=mesh['px'=16,'py'=16] {'px','py'}, use_global_device_ids=true, to_apply=%region_41.0 | all-reduce | flops 3 | bytes 24 | tf_op jit(solution)/shard_map/psum | solution.py:91
  1248.3 1.9 broadcast_select_fusion
  1250.2 3.6 multiply_reduce_fusion.4
  1255.2 73.7 %psum.141 = f32[]{:T(128)} all-reduce(f32[]{:T(128)} %multiply_reduce_fusion.4), channel_id=1, replica_groups=mesh['px'=16,'py'=16] {'px','py'}, use_global_device_ids=true, to_apply=%region_43.0 | all-reduce | flops 1 | bytes 8 | tf_op jit(solution)/shard_map/psum | solution.py:95
  1342.8 73.9 %all-reduce.20 = (f32[8]{0:T(128)S(1)}, f32[8]{0:T(128)S(1)}) all-reduce(f32[8]{0:T(128)S(1)} %get-tuple-element.148, f32[8]{0:T(128)S(1)} %get-tuple-element.147), channel_id=1, replica_groups=mesh['px'=16,'py'=16] {'px','py'}, use_global_device_ids=true, to_apply=%region_48.0 | all-reduce | flops 16 | bytes 128 | tf_op jit(solution)/shard_map/psum | solution.py:80
  1418.1 3.0 collective-permute-start.33
  1422.4 3.3 collective-permute-done.32
  1425.8 4.0 collective-permute-start.34
  1429.8 2.8 collective-permute-start.35
  (141 shorter events, 54.9 us)
Async XLA Ops:
  0.6 17.7 %copy-start = (f32[8,16,512]{2,1,0:T(8,128)S(1)}, f32[8,16,512]{2,1,0:T(8,128)}, u32[]{:S(2)}) copy-start(f32[8,16,512]{2,1,0:T(8,128)} %param.27) | copy-start | bytes 786436
  1.5 8.1 collective-permute-start
  2.8 5.8 collective-permute-start.1
  9.6 8.7 collective-permute-start.2
  15.1 3.2 collective-permute-start.3
  103.1 4.4 collective-permute-start.5
  105.5 4.7 collective-permute-start.4
  110.2 6.8 collective-permute-start.6
  114.2 3.5 collective-permute-start.7
  272.5 4.9 collective-permute-start.9
  274.9 4.7 collective-permute-start.8
  279.6 7.6 collective-permute-start.10
  283.6 3.7 collective-permute-start.11
  444.1 4.5 collective-permute-start.13
  446.4 4.7 collective-permute-start.12
  451.1 10.5 collective-permute-start.14
  455.1 6.5 collective-permute-start.15
  461.6 175.7 %copy-start.1 = (f32[8,8,16,512]{3,2,1,0:T(8,128)S(1)}, f32[8,8,16,512]{3,2,1,0:T(8,128)}, u32[]{:S(2)}) copy-start(f32[8,8,16,512]{3,2,1,0:T(8,128)} %param.28) | copy-start | bytes 6291460
  713.5 4.3 collective-permute-start.17
  716.5 4.7 collective-permute-start.16
  721.2 7.0 collective-permute-start.18
  725.2 3.7 collective-permute-start.19
  806.9 4.1 collective-permute-start.21
  809.8 4.7 collective-permute-start.20
  814.5 6.9 collective-permute-start.22
  818.5 3.7 collective-permute-start.23
  976.9 3.6 collective-permute-start.25
  979.2 4.7 collective-permute-start.24
  983.9 7.6 collective-permute-start.26
  987.9 3.7 collective-permute-start.27
  1148.4 4.6 collective-permute-start.29
  1150.8 4.7 collective-permute-start.28
  1156.1 10.4 collective-permute-start.30
  1160.1 6.4 collective-permute-start.31
  1418.1 16.4 %copy-start.2 = (f32[8,16,512]{2,1,0:T(8,128)}, f32[8,16,512]{2,1,0:T(8,128)S(1)}, u32[]{:S(2)}) copy-start(f32[8,16,512]{2,1,0:T(8,128)S(1)} %multiply_add_fusion) | copy-start | bytes 786436
  1418.1 4.3 collective-permute-start.33
  1421.1 4.7 collective-permute-start.32
  1425.8 7.0 collective-permute-start.34
  1429.8 3.7 collective-permute-start.35
where the time goes:
time: 1440 us; the launch traced here: 1430 us
  blocking collectives  1210 us (84%)
  starting transfers between devices  98.5 us (7%)
  other arithmetic  50.1 us (3%)
  between operations  27.2 us (2%)
  waiting for transfers between devices  26.3 us (2%)
  local copies, waits for them, and re-layouts  20.1 us (1%)
    psum x6, blocking collectives, local(): summed = lax.psum(heights_local, ('px', 'py'))  461 us
    psum x6, blocking collectives, local(): height = jnp.sqrt(lax.psum(jnp.sum(rest * rest), ('px', 'py')) + EPS)  443 us
    psum x4, blocking collectives, local(): lax.psum((dist_local, jnp.sum(force * force)), ('px', 'py'))  308 us
    ppermute x18, starting transfers between devices, extended(): lax.ppermute(tail, axis, [(i, (i + 1) % count) for i in range(ends)])  49.4 us
    ppermute x18, starting transfers between devices, extended(): lax.ppermute(head, axis, [((i + 1) % count, i) for i in range(ends)])  49.1 us
  transfers between devices with their start and end apart: 36, of which 14 were waited for; matrix products, arithmetic and copies ran while one was open for 1% of the time, Pallas kernels for 0%

commit v1 on v0

v1 whole, which is shorter than its diff:
```python
import jax
import jax.numpy as jnp
from jax import lax
from jax.experimental import pallas as pl
from jax.experimental.pallas import tpu as pltpu
from jax.sharding import PartitionSpec as P

EPS = 1e-06
DEFLATE = 4.0
ITERS = 3
KNOWN = 8
AXES = ("px", "py")
HX = 7
HY = 8
LANES = 128
F32 = jnp.float32

DIST, CROSS = 8, 16


def iotas():
    row = lax.broadcasted_iota(jnp.int32, (8, LANES), 0)
    lane = lax.broadcasted_iota(jnp.int32, (8, LANES), 1)
    return row, lane


def plane_sums(ref, x, tiles, ncol):
    row, lane = iotas()
    top = ref.shape[1] // 8
    zero = jnp.zeros((8, LANES), F32)
    need = range(max(tiles[0] - 1, 0), min(tiles[-1] + 2, top))
    v = {(t, c): ref[x, 8 * t:8 * t + 8, LANES * c:LANES * c + LANES] for t in need for c in range(ncol)}
    up = {(t, c): pltpu.roll(v[t, c], 1, 0) for t in need if t <= tiles[-1] for c in range(ncol)}
    down = {(t, c): pltpu.roll(v[t, c], 7, 0) for t in need if t >= tiles[0] for c in range(ncol)}
    out = {}
    for t in tiles:
        left = [pltpu.roll(v[t, c], 1, 1) for c in range(ncol)]
        right = [pltpu.roll(v[t, c], LANES - 1, 1) for c in range(ncol)]
        for c in range(ncol):
            rows, cols = slice(8 * t, 8 * t + 8), slice(LANES * c, LANES * c + LANES)
            a = up[t, c] if t == 0 else jnp.where(row == 0, up[t - 1, c], up[t, c])
            b = down[t, c] if t == top - 1 else jnp.where(row == 7, down[t + 1, c], down[t, c])
            l = jnp.where(lane == 0, left[c - 1] if c else zero, left[c])
            r = jnp.where(lane == LANES - 1, right[c + 1] if c < ncol - 1 else zero, right[c])
            total = (ref[x - 1, rows, cols] + ref[x + 1, rows, cols]) + (a + b) + (l + r)
            out[t, c] = (v[t, c], total)
    return out


def tile(t, c):
    return slice(8 * t, 8 * t + 8), slice(LANES * c, LANES * c + LANES)


def edges():
    ix, iy = lax.axis_index("px"), lax.axis_index("py")
    nx, ny = lax.axis_size("px"), lax.axis_size("py")
    flag = lambda cond: jnp.where(cond, 0.0, 1.0).astype(F32)
    return flag(ix == 0), flag(ix == nx - 1), flag(iy == 0), flag(iy == ny - 1)


def krylov(u_ref, w_refs, out_w, lo, hi, known_ref, sums_ref):
    ncol = u_ref.shape[2] // LANES
    planes = u_ref.shape[0]
    top = u_ref.shape[1] // 8
    x_lo, x_hi, y_lo, y_hi = edges()
    first, last = HX, planes - HX

    def mask(x):
        m = jnp.where(x < first, x_lo, jnp.where(x >= last, x_hi, 1.0))
        return m

    def stage(k):
        src = u_ref if k == 0 else w_refs[k - 1]
        dst = w_refs[k]

        def body(x, carry):
            m = mask(x)
            sums = plane_sums(src, x, list(range(top)), ncol)
            for (t, c), (v, total) in sums.items():
                rows, cols = tile(t, c)
                if k == 0:
                    value = 0.5 * total - v * (2.0 + v * v)
                else:
                    u = u_ref[x, rows, cols]
                    value = 0.5 * total + (1.0 - 3.0 * u * u) * v
                if t == 0:
                    value = value * (m * y_lo)
                elif t == top - 1:
                    value = value * (m * y_hi)
                else:
                    value = value * m
                dst[x, rows, cols] = value
            return carry

        lax.fori_loop(lo + k, hi - k, body, 0)

    for k in range(ITERS):
        stage(k)
    own = list(range(HY // 8, top - HY // 8))
    zero = jnp.zeros((8, LANES), F32)

    def moments(x, acc):
        acc = list(acc)
        sums = plane_sums(w_refs[2], x, own, ncol)
        for (t, c), (w2, total) in sums.items():
            rows, cols = tile(t, c)
            u = u_ref[x, rows, cols]
            w3 = 0.5 * total + (1.0 - 3.0 * u * u) * w2
            w0 = w_refs[0][x, rows, cols]
            w1 = w_refs[1][x, rows, cols]
            pairs = ((w0, w0), (w0, w1), (w1, w1), (w1, w2), (w2, w2), (w2, w3), (w3, w3))
            for n, (p, q) in enumerate(pairs):
                acc[n] = acc[n] + p * q
        return tuple(acc)

    acc = lax.fori_loop(first, last, moments, (zero,) * 7)

    def cross(x, acc):
        acc = list(acc)
        for t in own:
            for c in range(ncol):
                rows, cols = tile(t, c)
                u = u_ref[x, rows, cols]
                ws = [w_refs[m][x, rows, cols] for m in range(ITERS)]
                for i in range(KNOWN):
                    k = known_ref[i, x - first, slice(8 * t - HY, 8 * t - HY + 8), cols]
                    d = u - k
                    acc[i] = acc[i] + d * d
                    for m in range(ITERS):
                        acc[KNOWN * (m + 1) + i] = acc[KNOWN * (m + 1) + i] + d * ws[m]
        return tuple(acc)

    more = lax.fori_loop(first, last, cross, (zero,) * (KNOWN * (ITERS + 1)))
    parts = [jnp.sum(a, axis=0, keepdims=True) for a in (*acc, zero, *more)]
    block = jnp.concatenate(parts, axis=0)
    totals = jnp.sum(block, axis=1, keepdims=True)
    shape = block.shape
    hit = lax.broadcasted_iota(jnp.int32, shape, 0) == lax.broadcasted_iota(jnp.int32, shape, 1)
    line = jnp.sum(jnp.where(hit, totals, 0.0), axis=0, keepdims=True)
    sums_ref[...] = jnp.broadcast_to(line, sums_ref.shape)


def coefficients(recv_ref, cells):
    line = jnp.sum(recv_ref[...], axis=0, keepdims=True)
    line = jnp.broadcast_to(line, (8, LANES))
    mu = [jnp.broadcast_to(line[:, n:n + 1], (8, LANES)) for n in range(7)]
    zero = jnp.zeros((8, LANES), F32)

    def inner(p, q):
        total = None
        for i, a in enumerate(p):
            if a is None:
                continue
            part = None
            for j, b in enumerate(q):
                if b is None:
                    continue
                term = b * mu[i + j]
                part = term if part is None else part + term
            part = a * part
            total = part if total is None else total + part
        return total

    beta = jnp.sqrt(mu[0] + EPS)
    basis = [[-1.0 / beta]]
    hess = {}
    for k in range(ITERS):
        vec = basis[k]
        image = [None] * (k + 2)
        for i in range(k + 2):
            a = vec[i - 1] if i > 0 else None
            b = -3.0 * vec[i] if i <= k else None
            image[i] = b if a is None else (a if b is None else a + b)
        for j in range(k + 1):
            hess[j, k] = inner(basis[j], image)
        rest = list(image)
        for j in range(k + 1):
            for i in range(len(basis[j])):
                rest[i] = rest[i] - hess[j, k] * basis[j][i]
        square = jnp.maximum(inner(rest, rest), 0.0)
        hess[k + 1, k] = jnp.sqrt(square + EPS)
        if k < ITERS - 1:
            scale = 1.0 / hess[k + 1, k]
            basis.append([a * scale for a in rest])

    def normal(i, j):
        total = None
        for r in range(ITERS + 1):
            if (r, i) in hess and (r, j) in hess:
                term = hess[r, i] * hess[r, j]
                total = term if total is None else total + term
        return total

    lower = {}
    for j in range(ITERS):
        diag = normal(j, j)
        for r in range(j):
            diag = diag - lower[j, r] * lower[j, r]
        lower[j, j] = jnp.sqrt(diag)
        for i in range(j + 1, ITERS):
            off = normal(i, j)
            for r in range(j):
                off = off - lower[i, r] * lower[j, r]
            lower[i, j] = off / lower[j, j]
    forward = []
    for i in range(ITERS):
        part = beta * hess[0, i]
        for j in range(i):
            part = part - lower[i, j] * forward[j]
        forward.append(part / lower[i, i])
    back = [None] * ITERS
    for i in reversed(range(ITERS)):
        part = forward[i]
        for j in range(i + 1, ITERS):
            part = part - lower[j, i] * back[j]
        back[i] = part / lower[i, i]
    coef = []
    for m in range(ITERS):
        total = zero
        for j in range(m, ITERS):
            total = total + back[j] * basis[j][m]
        coef.append(total)
    lane = lax.broadcasted_iota(jnp.int32, (8, LANES), 1)
    dist = pltpu.roll(line, LANES - DIST, 1)
    dot = zero
    for m in range(ITERS):
        dot = dot + coef[m] * pltpu.roll(line, LANES - CROSS - KNOWN * m, 1)
    mean = dist / cells + EPS
    weight = 1.0 / mean + DEFLATE
    terms = jnp.where(lane < KNOWN, 2.0 * dot / (cells * mean * mean * weight), 0.0)
    total = jnp.sum(terms, axis=1, keepdims=True)
    tau = 1.0 / (1.0 + jnp.abs(jnp.broadcast_to(total, (8, LANES))))
    return [tau * a for a in coef]


def update(u_ref, w_refs, coef, dst, lo, hi):
    ncol = u_ref.shape[2] // LANES

    def body(x, carry):
        for t in range(u_ref.shape[1] // 8):
            for c in range(ncol):
                rows, cols = tile(t, c)
                value = u_ref[x, rows, cols]
                for a, w in zip(coef, w_refs):
                    value = value + a * w[x, rows, cols]
                dst[x, rows, cols] = value
        return carry

    lax.fori_loop(lo, hi, body, 0)


def first_kernel(mid_ref, lo_ref, hi_ref, known_hbm, u_ref, w0, w1, w2, sums_ref, known_ref, sems):
    inner = mid_ref.shape[0]
    copies = [
        pltpu.make_async_copy(lo_ref, u_ref.at[0:HX], sems.at[0]),
        pltpu.make_async_copy(mid_ref, u_ref.at[HX:HX + inner], sems.at[1]),
        pltpu.make_async_copy(hi_ref, u_ref.at[HX + inner:HX + inner + HX], sems.at[2]),
        pltpu.make_async_copy(known_hbm, known_ref, sems.at[3]),
    ]
    for copy in copies:
        copy.start()
    for copy in copies:
        copy.wait()
    planes = u_ref.shape[0]
    krylov(u_ref, (w0, w1, w2), None, 1, planes - 1, known_ref, sums_ref)


def second_kernel(cells, recv_ref, u_ref, a0, a1, a2, known_ref, v_ref, w0, w1, w2, sums_ref):
    coef = coefficients(recv_ref, cells)
    planes = u_ref.shape[0]
    update(u_ref, (a0, a1, a2), coef, v_ref, 3, planes - 3)
    krylov(v_ref, (w0, w1, w2), None, 4, planes - 4, known_ref, sums_ref)


def third_kernel(cells, recv_ref, u_ref, a0, a1, a2, out_ref, res_ref, v_ref):
    coef = coefficients(recv_ref, cells)
    planes = u_ref.shape[0]
    ncol = u_ref.shape[2] // LANES
    update(u_ref, (a0, a1, a2), coef, v_ref, HX - 1, planes - HX + 1)
    own = list(range(HY // 8, u_ref.shape[1] // 8 - HY // 8))

    def body(x, carry):
        for (t, c), (v, total) in plane_sums(v_ref, x, own, ncol).items():
            cols = slice(LANES * c, LANES * c + LANES)
            rows = slice(8 * t - HY, 8 * t - HY + 8)
            out_ref[x - HX, rows, cols] = v
            res_ref[x - HX, rows, cols] = 0.5 * total - v * (2.0 + v * v)
        return carry

    lax.fori_loop(HX, planes - HX, body, 0)


def total_over_devices(rows):
    count = rows.shape[0]
    rows = rows.reshape(count, 1, LANES)
    return lax.all_to_all(rows, AXES, 0, 0).reshape(count, LANES)


def shift(part, axis, step):
    count = lax.axis_size(axis)
    if step > 0:
        pairs = [(i, i + 1) for i in range(count - 1)]
    else:
        pairs = [(i + 1, i) for i in range(count - 1)]
    return lax.ppermute(part, axis, pairs)


def local(start_field, known):
    bx, by, bz = start_field.shape
    devices = lax.axis_size("px") * lax.axis_size("py")
    cells = float(bx * by * bz * devices)
    vmem = pl.BlockSpec(memory_space=pltpu.VMEM)
    hbm = pl.BlockSpec(memory_space=pl.ANY)
    params = pltpu.CompilerParams(vmem_limit_bytes=48 * 2**20)
    mid = jnp.concatenate(
        [shift(start_field[:, by - HY:], "py", 1), start_field, shift(start_field[:, :HY], "py", -1)], axis=1
    )
    lo = shift(mid[bx - HX:], "px", 1)
    hi = shift(mid[:HX], "px", -1)
    whole = jax.ShapeDtypeStruct((bx + 2 * HX, by + 2 * HY, bz), F32)
    sums = jax.ShapeDtypeStruct((devices, LANES), F32)
    own = jax.ShapeDtypeStruct((bx, by, bz), F32)
    u, a0, a1, a2, sent = pl.pallas_call(
        first_kernel,
        out_shape=(whole,) * 4 + (sums,),
        in_specs=[hbm] * 4,
        out_specs=(vmem,) * 5,
        scratch_shapes=[pltpu.VMEM(known.shape, F32), pltpu.SemaphoreType.DMA((4,))],
        compiler_params=params,
        name="first_step",
    )(mid, lo, hi, known)
    recv = total_over_devices(sent)
    v, b0, b1, b2, sent = pl.pallas_call(
        lambda *refs: second_kernel(cells, *refs),
        out_shape=(whole,) * 4 + (sums,),
        in_specs=[vmem] * 6,
        out_specs=(vmem,) * 5,
        compiler_params=params,
        name="second_step",
    )(recv, u, a0, a1, a2, known)
    recv = total_over_devices(sent)
    field, residual = pl.pallas_call(
        lambda *refs: third_kernel(cells, *refs),
        out_shape=(own, own),
        in_specs=[vmem] * 5,
        out_specs=(vmem, vmem),
        scratch_shapes=[pltpu.VMEM(whole.shape, F32)],
        compiler_params=params,
        name="finish",
    )(recv, v, b0, b1, b2)
    return field, residual


def solution(mesh):
    placed = (P("px", "py", None), P(None, "px", "py", None))
    return jax.shard_map(
        local,
        mesh=mesh,
        in_specs=placed,
        out_specs=(P("px", "py", None), P("px", "py", None)),
        check_vma=False,
    )
```

time: 1440 us -> 102 us (0.07)
  blocking collectives: 1210 us -> 50.1 us
  starting transfers between devices: 98.5 us -> 12.2 us
  other arithmetic: 50.1 us -> 0 us
  between operations: 27.2 us -> 0.73 us
  Pallas kernels: 0 us -> 21.9 us
  waiting for transfers between devices: 26.3 us -> 11.4 us
  local copies, waits for them, and re-layouts: 20.1 us -> 5.42 us
    psum x16 -> x0, blocking collectives: 1210 us -> none  [the longest x6 461 us: local(): summed = lax.psum(heights_local, ('px', 'py'))]
    ppermute x36 -> x4, starting transfers between devices: 98.5 us -> 12.2 us  [shift(): return lax.ppermute(part, axis, pairs)]
    all_to_all x0 -> x2, blocking collectives: none -> 50.1 us  [total_over_devices(): return lax.all_to_all(rows, AXES, 0, 0).reshape(count, LANES)]
    reduce_sum x20 -> x0, other arithmetic: 27.2 us -> none  [the longest x6 14 us: local(): height = jnp.sqrt(lax.psum(jnp.sum(rest * rest), ('px', 'py')) + EPS)]
    pallas_call x0 -> x3, Pallas kernels: none -> 21.9 us  [the longest x1 10.5 us: local(): pl.pallas_call(first_kernel, out_shape=(whole,) * 4 + (sums,), in_specs=[...]
    another operation x17 -> x0, other arithmetic: 18.3 us -> none
    ppermute x36 -> x4, waiting for transfers between devices: 26.3 us -> 11.4 us  [shift(): return lax.ppermute(part, axis, pairs)]
  transfers between devices with their start and end apart: 36 -> 4, of which waited for: 14 -> 3; matrix products, arithmetic and copies ran while one was open for 1% -> 1% of each run, Pallas kernels for 0% -> 0%
where the time goes in v1:
time: 102 us
  blocking collectives  50.1 us (49%)
  Pallas kernels  21.9 us (21%)
  starting transfers between devices  12.2 us (12%)
  waiting for transfers between devices  11.4 us (11%)
  local copies, waits for them, and re-layouts  5.42 us (5%)
    all_to_all x2, blocking collectives, total_over_devices(): return lax.all_to_all(rows, AXES, 0, 0).reshape(count, LANES)  50.1 us
    ppermute x4, starting transfers between devices, shift(): return lax.ppermute(part, axis, pairs)  12.2 us
    ppermute x4, waiting for transfers between devices, shift(): return lax.ppermute(part, axis, pairs)  11.4 us
    pallas_call x1, Pallas kernels, local(): pl.pallas_call(first_kernel, out_shape=(whole,) * 4 + (sums,), in_specs=[...  10.5 us
    pallas_call x1, Pallas kernels, local(): pl.pallas_call(lambda *refs: second_kernel(cells, *refs), out_shape=(whol...  9.41 us
    unnamed x8, local copies, waits for them, and re-layouts  4.33 us
  transfers between devices with their start and end apart: 4, of which 3 were waited for; matrix products, arithmetic and copies ran while one was open for 1% of the time, Pallas kernels for 0%

profile of v1, /device:TPU:1, one launch (start us, length us, event | category | flops | bytes accessed | tf_op | source)
XLA Modules:
  0.0 101.6 jit_solution(9721748085213529869)
XLA Ops:
  0.6 1.0 fusion.1
  1.6 4.9 %collective-permute-start = (f32[8,8,512]{2,1,0:T(8,128)S(1)}, f32[8,8,512]{2,1,0:T(8,128)S(1)}, u32[]{:S(2)}, u32[]{:S(2)}) collective-permute-start(f32[8,8,512]{2,1,0:T(8,128)S(1)} %get-tuple-element.25), channel_id=1, source_target_pairs={{0,1},{1,2},{2,3},{3,4},{4,5},{5,6},{6,7},{7,8},{8,9},{9,10},{10,1... | collective-permute-start | bytes 393224 | tf_op jit(solution)/shard_map/ppermute | solution.py:305
  6.6 1.9 %collective-permute-start.1 = (f32[8,8,512]{2,1,0:T(8,128)S(1)}, f32[8,8,512]{2,1,0:T(8,128)S(1)}, u32[]{:S(2)}, u32[]{:S(2)}) collective-permute-start(f32[8,8,512]{2,1,0:T(8,128)S(1)} %get-tuple-element.24), channel_id=1, source_target_pairs={{1,0},{2,1},{3,2},{4,3},{5,4},{6,5},{7,6},{8,7},{9,8},{10,9},{11,1... | collective-permute-start | bytes 393224 | tf_op jit(solution)/shard_map/ppermute | solution.py:305
  8.5 0.0 collective-permute-done
  8.5 1.0 constant_dynamic-update-slice_fusion.1
  9.5 3.4 %collective-permute-done.1 = f32[8,8,512]{2,1,0:T(8,128)S(1)} collective-permute-done((f32[8,8,512]{2,1,0:T(8,128)S(1)}, f32[8,8,512]{2,1,0:T(8,128)S(1)}, u32[]{:S(2)}, u32[]{:S(2)}) %collective-permute-start.1) | collective-permute-done | bytes 131104 | tf_op jit(solution)/shard_map/ppermute | solution.py:305
  12.9 0.1 fusion
  13.0 1.3 %collective-permute-start.3 = (f32[7,32,512]{2,1,0:T(8,128)S(1)}, f32[7,32,512]{2,1,0:T(8,128)S(1)}, u32[]{:S(2)}, u32[]{:S(2)}) collective-permute-start(f32[7,32,512]{2,1,0:T(8,128)S(1)} %get-tuple-element.22), channel_id=1, source_target_pairs={{16,0},{32,16},{48,32},{64,48},{80,64},{96,80},{112,96},{128,112},... | collective-permute-start | bytes 1376264 | tf_op jit(solution)/shard_map/ppermute | solution.py:305
  14.3 4.0 %collective-permute-start.2 = (f32[7,32,512]{2,1,0:T(8,128)S(1)}, f32[7,32,512]{2,1,0:T(8,128)S(1)}, u32[]{:S(2)}, u32[]{:S(2)}) collective-permute-start(f32[7,32,512]{2,1,0:T(8,128)S(1)} %get-tuple-element.23), channel_id=1, source_target_pairs={{0,16},{16,32},{32,48},{48,64},{64,80},{80,96},{96,112},{112,128},... | collective-permute-start | bytes 1376264 | tf_op jit(solution)/shard_map/ppermute | solution.py:305
  18.3 6.2 %collective-permute-done.3.hi_ref = f32[7,32,512]{2,1,0:T(8,128)S(1)} collective-permute-done((f32[7,32,512]{2,1,0:T(8,128)S(1)}, f32[7,32,512]{2,1,0:T(8,128)S(1)}, u32[]{:S(2)}, u32[]{:S(2)}) %collective-permute-start.3) | collective-permute-done | bytes 458784 | tf_op jit(solution)/shard_map/ppermute | solution.py:305
  24.5 1.8 %collective-permute-done.2.lo_ref = f32[7,32,512]{2,1,0:T(8,128)S(1)} collective-permute-done((f32[7,32,512]{2,1,0:T(8,128)S(1)}, f32[7,32,512]{2,1,0:T(8,128)S(1)}, u32[]{:S(2)}, u32[]{:S(2)}) %collective-permute-start.2) | collective-permute-done | bytes 458784 | tf_op jit(solution)/shard_map/ppermute | solution.py:305
  26.3 10.5 %first_step.1 = (f32[22,32,512]{2,1,0:T(8,128)S(1)}, f32[22,32,512]{2,1,0:T(8,128)S(1)}, f32[22,32,512]{2,1,0:T(8,128)S(1)}, f32[22,32,512]{2,1,0:T(8,128)}, f32[256,128]{1,0:T(8,128)S(1)}) custom-call(f32[8,32,512]{2,1,0:T(8,128)S(1)} %constant_dynamic-update-slice_fusion.mid_ref, f32[7,32,512]{2,1,0:T(8,128)S(1)} %collective-permute-done.2.lo_ref, ...), custom_call_target="tpu_custom_call" | custom-call | tf_op jit(solution)/shard_map/first_step/pallas_call | solution.py:323
  36.8 0.0 copy-start
  36.8 1.1 %copy-done = f32[22,32,512]{2,1,0:T(8,128)} copy-done((f32[22,32,512]{2,1,0:T(8,128)}, f32[22,32,512]{2,1,0:T(8,128)S(1)}, u32[]{:S(2)}) %copy-start) | copy-done | bytes 1441816
  37.9 0.0 copy-start.1
  37.9 1.1 %copy-done.1 = f32[22,32,512]{2,1,0:T(8,128)} copy-done((f32[22,32,512]{2,1,0:T(8,128)}, f32[22,32,512]{2,1,0:T(8,128)S(1)}, u32[]{:S(2)}) %copy-start.1) | copy-done | bytes 1441816
  39.0 0.0 copy-start.2
  39.0 1.1 %copy-done.2 = f32[22,32,512]{2,1,0:T(8,128)} copy-done((f32[22,32,512]{2,1,0:T(8,128)}, f32[22,32,512]{2,1,0:T(8,128)S(1)}, u32[]{:S(2)}) %copy-start.2) | copy-done | bytes 1441816
  40.2 31.5 %all_to_all.10 = f32[256,1,128]{2,1,0:T(1,128)S(1)} all-to-all(f32[256,1,128]{2,1,0:T(1,128)S(1)} %bitcast.11), channel_id=1, replica_groups=mesh['px'=16,'py'=16] {'px','py'}, dimensions={0} | all-to-all | bytes 262144 | tf_op jit(solution)/shard_map/all_to_all | solution.py:296
  71.7 9.4 %second_step.1 = (f32[22,32,512]{2,1,0:T(8,128)S(1)}, f32[22,32,512]{2,1,0:T(8,128)S(1)}, f32[22,32,512]{2,1,0:T(8,128)S(1)}, f32[22,32,512]{2,1,0:T(8,128)S(1)}, f32[256,128]{1,0:T(8,128)S(1)}) custom-call(f32[256,128]{1,0:T(8,128)S(1)} %bitcast.8, f32[22,32,512]{2,1,0:T(8,128)} %copy-done, f32[22,32,512]{2,1,0:T(8,128)} %copy-done.1, ...), custom_call_target="tpu_custom_call" | custom-call | tf_op jit(solution)/shard_map/second_step/pallas_call | solution.py:333
  81.1 18.6 %all_to_all.11 = f32[256,1,128]{2,1,0:T(1,128)S(1)} all-to-all(f32[256,1,128]{2,1,0:T(1,128)S(1)} %bitcast.10), channel_id=1, replica_groups=mesh['px'=16,'py'=16] {'px','py'}, dimensions={0} | all-to-all | bytes 262144 | tf_op jit(solution)/shard_map/all_to_all | solution.py:296
  99.7 1.9 %finish.1 = (f32[8,16,512]{2,1,0:T(8,128)}, f32[8,16,512]{2,1,0:T(8,128)}) custom-call(f32[256,128]{1,0:T(8,128)S(1)} %bitcast.9, f32[22,32,512]{2,1,0:T(8,128)S(1)} %get-tuple-element.18.refs_1_, f32[22,32,512]{2,1,0:T(8,128)S(1)} %get-tuple-element.19.refs_2_, f32[22,32,512]{2,1,0:T(8,128)S(1)} %get-tuple-element.20.refs_3_, ...), custom_call_target="tpu_custom_call" | custom-call | tf_op jit(solution)/shard_map/finish/pallas_call | solution.py:342
  (2 shorter events, 0.0 us)
Async XLA Ops:
  1.6 6.9 %collective-permute-start = (f32[8,8,512]{2,1,0:T(8,128)S(1)}, f32[8,8,512]{2,1,0:T(8,128)S(1)}, u32[]{:S(2)}, u32[]{:S(2)}) collective-permute-start(f32[8,8,512]{2,1,0:T(8,128)S(1)} %get-tuple-element.25), channel_id=1, source_target_pairs={{0,1},{1,2},{2,3},{3,4},{4,5},{5,6},{6,7},{7,8},{8,9},{9,10},{10,1... | collective-permute-start | bytes 393224 | tf_op jit(solution)/shard_map/ppermute | solution.py:305
  6.6 6.3 %collective-permute-start.1 = (f32[8,8,512]{2,1,0:T(8,128)S(1)}, f32[8,8,512]{2,1,0:T(8,128)S(1)}, u32[]{:S(2)}, u32[]{:S(2)}) collective-permute-start(f32[8,8,512]{2,1,0:T(8,128)S(1)} %get-tuple-element.24), channel_id=1, source_target_pairs={{1,0},{2,1},{3,2},{4,3},{5,4},{6,5},{7,6},{8,7},{9,8},{10,9},{11,1... | collective-permute-start | bytes 393224 | tf_op jit(solution)/shard_map/ppermute | solution.py:305
  13.0 11.6 %collective-permute-start.3 = (f32[7,32,512]{2,1,0:T(8,128)S(1)}, f32[7,32,512]{2,1,0:T(8,128)S(1)}, u32[]{:S(2)}, u32[]{:S(2)}) collective-permute-start(f32[7,32,512]{2,1,0:T(8,128)S(1)} %get-tuple-element.22), channel_id=1, source_target_pairs={{16,0},{32,16},{48,32},{64,48},{80,64},{96,80},{112,96},{128,112},... | collective-permute-start | bytes 1376264 | tf_op jit(solution)/shard_map/ppermute | solution.py:305
  14.3 12.0 %collective-permute-start.2 = (f32[7,32,512]{2,1,0:T(8,128)S(1)}, f32[7,32,512]{2,1,0:T(8,128)S(1)}, u32[]{:S(2)}, u32[]{:S(2)}) collective-permute-start(f32[7,32,512]{2,1,0:T(8,128)S(1)} %get-tuple-element.23), channel_id=1, source_target_pairs={{0,16},{16,32},{32,48},{48,64},{64,80},{80,96},{96,112},{112,128},... | collective-permute-start | bytes 1376264 | tf_op jit(solution)/shard_map/ppermute | solution.py:305
  36.8 1.1 %copy-start = (f32[22,32,512]{2,1,0:T(8,128)}, f32[22,32,512]{2,1,0:T(8,128)S(1)}, u32[]{:S(2)}) copy-start(f32[22,32,512]{2,1,0:T(8,128)S(1)} %get-tuple-element.13.refs_1_) | copy-start | bytes 4325380
  37.9 1.1 %copy-start.1 = (f32[22,32,512]{2,1,0:T(8,128)}, f32[22,32,512]{2,1,0:T(8,128)S(1)}, u32[]{:S(2)}) copy-start(f32[22,32,512]{2,1,0:T(8,128)S(1)} %get-tuple-element.14.refs_2_) | copy-start | bytes 4325380
  39.0 1.1 %copy-start.2 = (f32[22,32,512]{2,1,0:T(8,128)}, f32[22,32,512]{2,1,0:T(8,128)S(1)}, u32[]{:S(2)}) copy-start(f32[22,32,512]{2,1,0:T(8,128)S(1)} %get-tuple-element.15.refs_3_) | copy-start | bytes 4325380

commit v2 on v1

--- a/solution.py
+++ b/solution.py
@@ -34,17 +34,36 @@
     down = {(t, c): pltpu.roll(v[t, c], 7, 0) for t in need if t >= tiles[0] for c in range(ncol)}
     out = {}
     for t in tiles:
-        left = [pltpu.roll(v[t, c], 1, 1) for c in range(ncol)]
-        right = [pltpu.roll(v[t, c], LANES - 1, 1) for c in range(ncol)]
+        before = jnp.where(lane == 0, zero, pltpu.roll(v[t, ncol - 1], 1, 1))
+        after = jnp.where(lane == LANES - 1, zero, pltpu.roll(v[t, 0], LANES - 1, 1))
         for c in range(ncol):
-            rows, cols = slice(8 * t, 8 * t + 8), slice(LANES * c, LANES * c + LANES)
+            rows, cols = tile(t, c)
             a = up[t, c] if t == 0 else jnp.where(row == 0, up[t - 1, c], up[t, c])
             b = down[t, c] if t == top - 1 else jnp.where(row == 7, down[t + 1, c], down[t, c])
-            l = jnp.where(lane == 0, left[c - 1] if c else zero, left[c])
-            r = jnp.where(lane == LANES - 1, right[c + 1] if c < ncol - 1 else zero, right[c])
+            l = v[t, c - 1] if c else before
+            r = v[t, c + 1] if c < ncol - 1 else after
             total = (ref[x - 1, rows, cols] + ref[x + 1, rows, cols]) + (a + b) + (l + r)
             out[t, c] = (v[t, c], total)
     return out
+
+
+def interleave(width, back):
+    ncol = width // LANES
+    dim_z, dim_p = (1, 0) if back else (0, 1)
+    z = lax.broadcasted_iota(jnp.int32, (width, width), dim_z)
+    p = lax.broadcasted_iota(jnp.int32, (width, width), dim_p)
+    hit = z == (p % LANES) * ncol + p // LANES
+    return jnp.where(hit, 1.0, 0.0).astype(jnp.bfloat16)
+
+
+def move(value, matrix):
+    total = None
+    for _ in range(3):
+        part = value.astype(jnp.bfloat16)
+        value = value - part.astype(F32)
+        piece = jnp.dot(part, matrix, preferred_element_type=F32)
+        total = piece if total is None else total + piece
+    return total
 
 
 def tile(t, c):
@@ -58,7 +77,7 @@
     return flag(ix == 0), flag(ix == nx - 1), flag(iy == 0), flag(iy == ny - 1)
 
 
-def krylov(u_ref, w_refs, out_w, lo, hi, known_ref, sums_ref):
+def krylov(u_ref, w_refs, lo, hi, known_ref, sums_ref):
     ncol = u_ref.shape[2] // LANES
     planes = u_ref.shape[0]
     top = u_ref.shape[1] // 8
@@ -79,10 +98,10 @@
             for (t, c), (v, total) in sums.items():
                 rows, cols = tile(t, c)
                 if k == 0:
-                    value = 0.5 * total - v * (2.0 + v * v)
+                    value = total - v * (4.0 + 2.0 * (v * v))
                 else:
                     u = u_ref[x, rows, cols]
-                    value = 0.5 * total + (1.0 - 3.0 * u * u) * v
+                    value = total + (2.0 - 6.0 * (u * u)) * v
                 if t == 0:
                     value = value * (m * y_lo)
                 elif t == top - 1:
@@ -105,7 +124,7 @@
         for (t, c), (w2, total) in sums.items():
             rows, cols = tile(t, c)
             u = u_ref[x, rows, cols]
-            w3 = 0.5 * total + (1.0 - 3.0 * u * u) * w2
+            w3 = total + (2.0 - 6.0 * (u * u)) * w2
             w0 = w_refs[0][x, rows, cols]
             w1 = w_refs[1][x, rows, cols]
             pairs = ((w0, w0), (w0, w1), (w1, w1), (w1, w2), (w2, w2), (w2, w3), (w3, w3))
@@ -161,14 +180,14 @@
             total = part if total is None else total + part
         return total
 
-    beta = jnp.sqrt(mu[0] + EPS)
-    basis = [[-1.0 / beta]]
+    beta = jnp.sqrt(0.25 * mu[0] + EPS)
+    basis = [[-0.5 / beta]]
     hess = {}
     for k in range(ITERS):
         vec = basis[k]
         image = [None] * (k + 2)
         for i in range(k + 2):
-            a = vec[i - 1] if i > 0 else None
+            a = 0.5 * vec[i - 1] if i > 0 else None
             b = -3.0 * vec[i] if i <= k else None
             image[i] = b if a is None else (a if b is None else a + b)
         for j in range(k + 1):
@@ -249,30 +268,71 @@
     lax.fori_loop(lo, hi, body, 0)
 
 
-def first_kernel(mid_ref, lo_ref, hi_ref, known_hbm, u_ref, w0, w1, w2, sums_ref, known_ref, sems):
-    inner = mid_ref.shape[0]
-    copies = [
-        pltpu.make_async_copy(lo_ref, u_ref.at[0:HX], sems.at[0]),
-        pltpu.make_async_copy(mid_ref, u_ref.at[HX:HX + inner], sems.at[1]),
-        pltpu.make_async_copy(hi_ref, u_ref.at[HX + inner:HX + inner + HX], sems.at[2]),
-        pltpu.make_async_copy(known_hbm, known_ref, sems.at[3]),
-    ]
-    for copy in copies:
-        copy.start()
-    for copy in copies:
-        copy.wait()
-    planes = u_ref.shape[0]
-    krylov(u_ref, (w0, w1, w2), None, 1, planes - 1, known_ref, sums_ref)
+def parity(axis):
+    return lax.axis_index(axis) % 2
+
+
+def spread_kernel(field_hbm, out_ref, first_ref, second_ref, field_ref, sem):
+    copy = pltpu.make_async_copy(field_hbm, field_ref, sem)
+    copy.start()
+    bx, by, bz = out_ref.shape
+    matrix = interleave(bz, False)
+    copy.wait()
+    out_ref[...] = move(field_ref[...].reshape(bx * by, bz), matrix).reshape(bx, by, bz)
+    odd = parity("px")
+    first_ref[...] = out_ref[pl.ds(1 - odd, HX)]
+    second_ref[...] = out_ref[pl.ds(odd, HX)]
+
+
+def known_kernel(known_ref, out_ref, back_ref):
+    shape = known_ref.shape
+    bz = shape[-1]
+    matrix = interleave(bz, False)
+    for i in range(shape[0]):
+        part = move(known_ref[i].reshape(-1, bz), matrix)
+        out_ref[i] = part.reshape(shape[1:])
+    back_ref[...] = interleave(bz, True)
+
+
+def join_kernel(own_ref, first_ref, second_ref, mid_ref, up_ref, down_ref):
+    bx, by, bz = own_ref.shape
+    odd = parity("px")
+    mid_ref[pl.ds((1 - odd) * (HX + bx), HX)] = first_ref[...]
+    mid_ref[pl.ds(odd * (HX + bx), HX)] = second_ref[...]
+    mid_ref[HX:HX + bx] = own_ref[...]
+    odd = parity("py")
+    count = up_ref.shape[0]
+    high = pl.multiple_of((1 - odd) * (by - HY), HY)
+    low = pl.multiple_of(odd * (by - HY), HY)
+    up_ref[...] = mid_ref[1:1 + count, pl.ds(high, HY)]
+    down_ref[...] = mid_ref[1:1 + count, pl.ds(low, HY)]
+
+
+def first_kernel(mid_ref, up_ref, down_ref, known_ref, u_ref, w0, w1, w2, sums_ref):
+    planes, rows, bz = u_ref.shape
+    by = rows - 2 * HY
+    count = up_ref.shape[0]
+    odd = parity("py")
+    edge = jnp.zeros((1, HY, bz), F32)
+    for x in (0, planes - 1):
+        for y in (0, HY + by):
+            u_ref[x:x + 1, y:y + HY] = edge
+    u_ref[:, HY:HY + by] = mid_ref[...]
+    high = pl.multiple_of((1 - odd) * (HY + by), HY)
+    low = pl.multiple_of(odd * (HY + by), HY)
+    u_ref[1:1 + count, pl.ds(high, HY)] = up_ref[...]
+    u_ref[1:1 + count, pl.ds(low, HY)] = down_ref[...]
+    krylov(u_ref, (w0, w1, w2), 1, planes - 1, known_ref, sums_ref)
 
 
 def second_kernel(cells, recv_ref, u_ref, a0, a1, a2, known_ref, v_ref, w0, w1, w2, sums_ref):
     coef = coefficients(recv_ref, cells)
     planes = u_ref.shape[0]
     update(u_ref, (a0, a1, a2), coef, v_ref, 3, planes - 3)
-    krylov(v_ref, (w0, w1, w2), None, 4, planes - 4, known_ref, sums_ref)
-
-
-def third_kernel(cells, recv_ref, u_ref, a0, a1, a2, out_ref, res_ref, v_ref):
+    krylov(v_ref, (w0, w1, w2), 4, planes - 4, known_ref, sums_ref)
+
+
+def third_kernel(cells, recv_ref, u_ref, a0, a1, a2, back_ref, out_ref, res_ref, v_ref, f_ref):
     coef = coefficients(recv_ref, cells)
     planes = u_ref.shape[0]
     ncol = u_ref.shape[2] // LANES
@@ -283,11 +343,15 @@
         for (t, c), (v, total) in plane_sums(v_ref, x, own, ncol).items():
             cols = slice(LANES * c, LANES * c + LANES)
             rows = slice(8 * t - HY, 8 * t - HY + 8)
-            out_ref[x - HX, rows, cols] = v
-            res_ref[x - HX, rows, cols] = 0.5 * total - v * (2.0 + v * v)
+            f_ref[x - HX, rows, cols] = 0.5 * total - v * (2.0 + v * v)
         return carry
 
     lax.fori_loop(HX, planes - HX, body, 0)
+    shape = out_ref.shape
+    back = back_ref[...]
+    mine = v_ref[HX:HX + shape[0], HY:HY + shape[1]]
+    out_ref[...] = move(mine.reshape(-1, shape[2]), back).reshape(shape)
+    res_ref[...] = move(f_ref[...].reshape(-1, shape[2]), back).reshape(shape)
 
 
 def total_over_devices(rows):
@@ -296,12 +360,10 @@
     return lax.all_to_all(rows, AXES, 0, 0).reshape(count, LANES)
 
 
-def shift(part, axis, step):
-    count = lax.axis_size(axis)
-    if step > 0:
-        pairs = [(i, i + 1) for i in range(count - 1)]
-    else:
-        pairs = [(i + 1, i) for i in range(count - 1)]
+def swap(part, axis, first):
+    pairs = []
+    for i in range(first, lax.axis_size(axis) - 1, 2):
+        pairs += [(i, i + 1), (i + 1, i)]
     return lax.ppermute(part, axis, pairs)
 
 
@@ -311,43 +373,53 @@
     cells = float(bx * by * bz * devices)
     vmem = pl.BlockSpec(memory_space=pltpu.VMEM)
     hbm = pl.BlockSpec(memory_space=pl.ANY)
-    params = pltpu.CompilerParams(vmem_limit_bytes=48 * 2**20)
-    mid = jnp.concatenate(
-        [shift(start_field[:, by - HY:], "py", 1), start_field, shift(start_field[:, :HY], "py", -1)], axis=1
+    params = pltpu.CompilerParams(vmem_limit_bytes=24 * 2**20)
+    shape = lambda *dims: jax.ShapeDtypeStruct(dims, F32)
+
+    def call(body, name, outs, *args, specs=None, scratch=()):
+        return pl.pallas_call(
+            body,
+            out_shape=outs,
+            in_specs=[vmem] * len(args) if specs is None else specs,
+            out_specs=tuple(vmem for _ in outs),
+            scratch_shapes=scratch,
+            compiler_params=params,
+            name=name,
+        )(*args)
+
+    planes, rows = bx + 2 * HX, by + 2 * HY
+    side = shape(HX, by, bz)
+    mine, first, second = call(
+        spread_kernel,
+        "spread",
+        (shape(bx, by, bz), side, side),
+        start_field,
+        specs=[hbm],
+        scratch=[pltpu.VMEM((bx, by, bz), F32), pltpu.SemaphoreType.DMA],
     )
-    lo = shift(mid[bx - HX:], "px", 1)
-    hi = shift(mid[:HX], "px", -1)
-    whole = jax.ShapeDtypeStruct((bx + 2 * HX, by + 2 * HY, bz), F32)
-    sums = jax.ShapeDtypeStruct((devices, LANES), F32)
-    own = jax.ShapeDtypeStruct((bx, by, bz), F32)
-    u, a0, a1, a2, sent = pl.pallas_call(
-        first_kernel,
-        out_shape=(whole,) * 4 + (sums,),
-        in_specs=[hbm] * 4,
-        out_specs=(vmem,) * 5,
-        scratch_shapes=[pltpu.VMEM(known.shape, F32), pltpu.SemaphoreType.DMA((4,))],
+    first, second = swap(first, "px", 0), swap(second, "px", 1)
+    known, back = pl.pallas_call(
+        known_kernel,
+        out_shape=(jax.ShapeDtypeStruct(known.shape, F32), jax.ShapeDtypeStruct((bz, bz), jnp.bfloat16)),
+        in_specs=[vmem],
+        out_specs=(vmem, vmem),
         compiler_params=params,
-        name="first_step",
-    )(mid, lo, hi, known)
+        name="known_spread",
+    )(known)
+    strip = shape(planes - 2, HY, bz)
+    mid, up, down = call(join_kernel, "join", (shape(planes, by, bz), strip, strip), mine, first, second)
+    up, down = swap(up, "py", 0), swap(down, "py", 1)
+    whole = shape(planes, rows, bz)
+    sums = shape(devices, LANES)
+    own = shape(bx, by, bz)
+    u, a0, a1, a2, sent = call(first_kernel, "first_step", (whole,) * 4 + (sums,), mid, up, down, known)
     recv = total_over_devices(sent)
-    v, b0, b1, b2, sent = pl.pallas_call(
-        lambda *refs: second_kernel(cells, *refs),
-        out_shape=(whole,) * 4 + (sums,),
-        in_specs=[vmem] * 6,
-        out_specs=(vmem,) * 5,
-        compiler_params=params,
-        name="second_step",
-    )(recv, u, a0, a1, a2, known)
+    body = lambda *refs: second_kernel(cells, *refs)
+    v, b0, b1, b2, sent = call(body, "second_step", (whole,) * 4 + (sums,), recv, u, a0, a1, a2, known)
     recv = total_over_devices(sent)
-    field, residual = pl.pallas_call(
-        lambda *refs: third_kernel(cells, *refs),
-        out_shape=(own, own),
-        in_specs=[vmem] * 5,
-        out_specs=(vmem, vmem),
-        scratch_shapes=[pltpu.VMEM(whole.shape, F32)],
-        compiler_params=params,
-        name="finish",
-    )(recv, v, b0, b1, b2)
+    body = lambda *refs: third_kernel(cells, *refs)
+    scratch = [pltpu.VMEM(whole.shape, F32), pltpu.VMEM(own.shape, F32)]
+    field, residual = call(body, "finish", (own, own), recv, v, b0, b1, b2, back, scratch=scratch)
     return field, residual
 
 

time: 102 us -> 84.5 us (0.83)
  waiting for transfers between devices: 11.4 us -> 5.08 us
  Pallas kernels: 21.9 us -> 16.2 us
  starting transfers between devices: 12.2 us -> 9.14 us
  local copies, waits for them, and re-layouts: 5.42 us -> 2.53 us
    ppermute x4, waiting for transfers between devices: 11.4 us -> 5.08 us  [swap(): return lax.ppermute(part, axis, pairs)]
    pallas_call x3 -> x6, Pallas kernels: 21.9 us -> 16.2 us  [the longest x5 14.3 us: call(): pl.pallas_call(body, out_shape=outs, in_specs=[vmem] * len(args) if specs...]
    ppermute x4, starting transfers between devices: 12.2 us -> 9.14 us  [swap(): return lax.ppermute(part, axis, pairs)]
    unnamed x8 -> x4, local copies, waits for them, and re-layouts: 4.33 us -> 2.53 us
    slice x2 -> x0, local copies, waits for them, and re-layouts: 1.09 us -> none  [the longest x1 0.99 us: local(): start_field[:, :HY]]
  transfers between devices with their start and end apart: 4 -> 4, of which waited for: 3 -> 2; matrix products, arithmetic and copies ran while one was open for 1% -> 0% of each run, Pallas kernels for 0% -> 2%
where the time goes in v2:
time: 84.5 us; the launch traced here: 84.2 us
  blocking collectives  50.6 us (60%)
  Pallas kernels  16.2 us (19%)
  starting transfers between devices  9.14 us (11%)
  waiting for transfers between devices  5.08 us (6%)
  local copies, waits for them, and re-layouts  2.53 us (3%)
    all_to_all x2, blocking collectives, total_over_devices(): return lax.all_to_all(rows, AXES, 0, 0).reshape(count, LANES)  50.6 us
    pallas_call x5, Pallas kernels, call(): pl.pallas_call(body, out_shape=outs, in_specs=[vmem] * len(args) if specs...  14.3 us
    ppermute x4, starting transfers between devices, swap(): return lax.ppermute(part, axis, pairs)  9.14 us
    ppermute x4, waiting for transfers between devices, swap(): return lax.ppermute(part, axis, pairs)  5.08 us
    unnamed x4, local copies, waits for them, and re-layouts  2.53 us
    pallas_call x1, Pallas kernels, local(): pl.pallas_call(known_kernel, out_shape=(jax.ShapeDtypeStruct(known.shape,...  1.97 us
  transfers between devices with their start and end apart: 4, of which 2 were waited for; matrix products, arithmetic and copies ran while one was open for 0% of the time, Pallas kernels for 2%

profile of v2, /device:TPU:1, one launch (start us, length us, event | category | flops | bytes accessed | tf_op | source)
XLA Modules:
  0.0 84.2 jit_solution(12886558197753182499)
XLA Ops:
  0.6 0.0 copy-start.1
  0.6 0.9 %copy-done.1 = f32[8,16,512]{2,1,0:T(8,128)S(1)} copy-done((f32[8,16,512]{2,1,0:T(8,128)S(1)}, f32[8,16,512]{2,1,0:T(8,128)}, u32[]{:S(2)}) %copy-start.1) | copy-done | bytes 262168
  1.6 0.6 spread.1
  2.2 2.1 %collective-permute-start = (f32[7,16,512]{2,1,0:T(8,128)S(1)}, f32[7,16,512]{2,1,0:T(8,128)S(1)}, u32[]{:S(2)}, u32[]{:S(2)}) collective-permute-start(f32[7,16,512]{2,1,0:T(8,128)S(1)} %get-tuple-element.21), channel_id=1, source_target_pairs={{0,16},{16,0},{32,48},{48,32},{64,80},{80,64},{96,112},{112,96},{1... | collective-permute-start | bytes 688136 | tf_op jit(solution)/shard_map/ppermute | solution.py:367
  4.3 0.7 collective-permute-start.1
  5.0 3.3 %collective-permute-done.first_ref = f32[7,16,512]{2,1,0:T(8,128)S(1)} collective-permute-done((f32[7,16,512]{2,1,0:T(8,128)S(1)}, f32[7,16,512]{2,1,0:T(8,128)S(1)}, u32[]{:S(2)}, u32[]{:S(2)}) %collective-permute-start) | collective-permute-done | bytes 229408 | tf_op jit(solution)/shard_map/ppermute | solution.py:367
  8.3 0.0 collective-permute-done.1.second_ref
  8.3 0.1 join.1
  8.4 3.3 %collective-permute-start.2 = (f32[20,8,512]{2,1,0:T(8,128)S(1)}, f32[20,8,512]{2,1,0:T(8,128)S(1)}, u32[]{:S(2)}, u32[]{:S(2)}) collective-permute-start(f32[20,8,512]{2,1,0:T(8,128)S(1)} %get-tuple-element.24), channel_id=1, source_target_pairs={{0,1},{1,0},{2,3},{3,2},{4,5},{5,4},{6,7},{7,6},{8,9},{9,8},{10,11... | collective-permute-start | bytes 983048 | tf_op jit(solution)/shard_map/ppermute | solution.py:367
  11.8 3.0 %collective-permute-start.3 = (f32[20,8,512]{2,1,0:T(8,128)S(1)}, f32[20,8,512]{2,1,0:T(8,128)S(1)}, u32[]{:S(2)}, u32[]{:S(2)}) collective-permute-start(f32[20,8,512]{2,1,0:T(8,128)S(1)} %get-tuple-element.25), channel_id=1, source_target_pairs={{1,2},{2,1},{3,4},{4,3},{5,6},{6,5},{7,8},{8,7},{9,10},{10,9},{11,... | collective-permute-start | bytes 983048 | tf_op jit(solution)/shard_map/ppermute | solution.py:367
  14.8 0.0 copy-start
  14.8 1.6 %copy-done = f32[8,8,16,512]{3,2,1,0:T(8,128)S(1)} copy-done((f32[8,8,16,512]{3,2,1,0:T(8,128)S(1)}, f32[8,8,16,512]{3,2,1,0:T(8,128)}, u32[]{:S(2)}) %copy-start) | copy-done | bytes 2097176
  16.4 2.0 %known_spread.1 = (f32[8,8,16,512]{3,2,1,0:T(8,128)S(1)}, bf16[512,512]{1,0:T(8,128)(2,1)S(1)}) custom-call(f32[8,8,16,512]{3,2,1,0:T(8,128)S(1)} %copy-done), custom_call_target="tpu_custom_call" | custom-call | tf_op jit(solution)/shard_map/known_spread/pallas_call | solution.py:401
  18.4 0.0 collective-permute-done.2.up_ref
  18.4 1.8 %collective-permute-done.3.down_ref = f32[20,8,512]{2,1,0:T(8,128)S(1)} collective-permute-done((f32[20,8,512]{2,1,0:T(8,128)S(1)}, f32[20,8,512]{2,1,0:T(8,128)S(1)}, u32[]{:S(2)}, u32[]{:S(2)}) %collective-permute-start.3) | collective-permute-done | bytes 327712 | tf_op jit(solution)/shard_map/ppermute | solution.py:367
  20.1 6.0 %first_step.1 = (f32[22,32,512]{2,1,0:T(8,128)S(1)}, f32[22,32,512]{2,1,0:T(8,128)S(1)}, f32[22,32,512]{2,1,0:T(8,128)S(1)}, f32[22,32,512]{2,1,0:T(8,128)S(1)}, f32[256,128]{1,0:T(8,128)S(1)}) custom-call(f32[22,16,512]{2,1,0:T(8,128)S(1)} %get-tuple-element.23.mid_ref, f32[20,8,512]{2,1,0:T(8,128)S(1)} %collective-permute-done.2.up_ref, ...), custom_call_target="tpu_custom_call" | custom-call | tf_op jit(solution)/shard_map/first_step/pallas_call | solution.py:380
  26.2 31.9 %all_to_all.10 = f32[256,1,128]{2,1,0:T(1,128)S(1)} all-to-all(f32[256,1,128]{2,1,0:T(1,128)S(1)} %bitcast.11), channel_id=1, replica_groups=mesh['px'=16,'py'=16] {'px','py'}, dimensions={0} | all-to-all | bytes 262144 | tf_op jit(solution)/shard_map/all_to_all | solution.py:360
  58.1 5.1 %second_step.1 = (f32[22,32,512]{2,1,0:T(8,128)S(1)}, f32[22,32,512]{2,1,0:T(8,128)S(1)}, f32[22,32,512]{2,1,0:T(8,128)S(1)}, f32[22,32,512]{2,1,0:T(8,128)S(1)}, f32[256,128]{1,0:T(8,128)S(1)}) custom-call(f32[256,128]{1,0:T(8,128)S(1)} %bitcast.8, f32[22,32,512]{2,1,0:T(8,128)S(1)} %get-tuple-element.28.refs_1_, ...), custom_call_target="tpu_custom_call" | custom-call | tf_op jit(solution)/shard_map/second_step/pallas_call | solution.py:380
  63.2 18.6 %all_to_all.11 = f32[256,1,128]{2,1,0:T(1,128)S(1)} all-to-all(f32[256,1,128]{2,1,0:T(1,128)S(1)} %bitcast.10), channel_id=1, replica_groups=mesh['px'=16,'py'=16] {'px','py'}, dimensions={0} | all-to-all | bytes 262144 | tf_op jit(solution)/shard_map/all_to_all | solution.py:360
  81.8 2.4 %finish.1 = (f32[8,16,512]{2,1,0:T(8,128)}, f32[8,16,512]{2,1,0:T(8,128)}) custom-call(f32[256,128]{1,0:T(8,128)S(1)} %bitcast.9, f32[22,32,512]{2,1,0:T(8,128)S(1)} %get-tuple-element.33.refs_1_, f32[22,32,512]{2,1,0:T(8,128)S(1)} %get-tuple-element.34.refs_2_, f32[22,32,512]{2,1,0:T(8,128)S(1)} %get-tuple-element.35.refs_3_, ...), custom_call_target="tpu_custom_call" | custom-call | tf_op jit(solution)/shard_map/finish/pallas_call | solution.py:380
Async XLA Ops:
  0.6 1.0 %copy-start.1 = (f32[8,16,512]{2,1,0:T(8,128)S(1)}, f32[8,16,512]{2,1,0:T(8,128)}, u32[]{:S(2)}) copy-start(f32[8,16,512]{2,1,0:T(8,128)} %field_hbm.1) | copy-start | bytes 786436
  2.2 6.1 %collective-permute-start = (f32[7,16,512]{2,1,0:T(8,128)S(1)}, f32[7,16,512]{2,1,0:T(8,128)S(1)}, u32[]{:S(2)}, u32[]{:S(2)}) collective-permute-start(f32[7,16,512]{2,1,0:T(8,128)S(1)} %get-tuple-element.21), channel_id=1, source_target_pairs={{0,16},{16,0},{32,48},{48,32},{64,80},{80,64},{96,112},{112,96},{1... | collective-permute-start | bytes 688136 | tf_op jit(solution)/shard_map/ppermute | solution.py:367
  4.3 4.0 %collective-permute-start.1 = (f32[7,16,512]{2,1,0:T(8,128)S(1)}, f32[7,16,512]{2,1,0:T(8,128)S(1)}, u32[]{:S(2)}, u32[]{:S(2)}) collective-permute-start(f32[7,16,512]{2,1,0:T(8,128)S(1)} %get-tuple-element.22), channel_id=1, source_target_pairs={{16,32},{32,16},{48,64},{64,48},{80,96},{96,80},{112,128},{128,112... | collective-permute-start | bytes 688136 | tf_op jit(solution)/shard_map/ppermute | solution.py:367
  8.4 9.9 %collective-permute-start.2 = (f32[20,8,512]{2,1,0:T(8,128)S(1)}, f32[20,8,512]{2,1,0:T(8,128)S(1)}, u32[]{:S(2)}, u32[]{:S(2)}) collective-permute-start(f32[20,8,512]{2,1,0:T(8,128)S(1)} %get-tuple-element.24), channel_id=1, source_target_pairs={{0,1},{1,0},{2,3},{3,2},{4,5},{5,4},{6,7},{7,6},{8,9},{9,8},{10,11... | collective-permute-start | bytes 983048 | tf_op jit(solution)/shard_map/ppermute | solution.py:367
  11.8 8.4 %collective-permute-start.3 = (f32[20,8,512]{2,1,0:T(8,128)S(1)}, f32[20,8,512]{2,1,0:T(8,128)S(1)}, u32[]{:S(2)}, u32[]{:S(2)}) collective-permute-start(f32[20,8,512]{2,1,0:T(8,128)S(1)} %get-tuple-element.25), channel_id=1, source_target_pairs={{1,2},{2,1},{3,4},{4,3},{5,6},{6,5},{7,8},{8,7},{9,10},{10,9},{11,... | collective-permute-start | bytes 983048 | tf_op jit(solution)/shard_map/ppermute | solution.py:367
  14.8 1.6 %copy-start = (f32[8,8,16,512]{3,2,1,0:T(8,128)S(1)}, f32[8,8,16,512]{3,2,1,0:T(8,128)}, u32[]{:S(2)}) copy-start(f32[8,8,16,512]{3,2,1,0:T(8,128)} %known_ref.1) | copy-start | bytes 6291460

commit v3 on v2

v3 whole, which is shorter than its diff:
```python
import jax
import jax.numpy as jnp
from jax import lax
from jax.experimental import pallas as pl
from jax.experimental.pallas import tpu as pltpu
from jax.sharding import PartitionSpec as P

EPS = 1e-06
DEFLATE = 4.0
ITERS = 3
KNOWN = 8
AXES = ("px", "py")
HX = 7
HY = 8
LANES = 128
F32 = jnp.float32

DIST, CROSS = 8, 16


def iotas():
    row = lax.broadcasted_iota(jnp.int32, (8, LANES), 0)
    lane = lax.broadcasted_iota(jnp.int32, (8, LANES), 1)
    return row, lane


def plane_sums(ref, x, tiles):
    row, lane = iotas()
    top, ncol = ref.shape[1] // 8, ref.shape[2] // LANES
    zero = jnp.zeros((8, LANES), F32)
    need = range(max(tiles[0] - 1, 0), min(tiles[-1] + 2, top))
    v = {(t, c): ref[(x, *tile(t, c))] for t in need for c in range(ncol)}
    up = {(t, c): pltpu.roll(v[t, c], 1, 0) for t in need if t <= tiles[-1] for c in range(ncol)}
    down = {(t, c): pltpu.roll(v[t, c], 7, 0) for t in need if t >= tiles[0] for c in range(ncol)}
    for t in tiles:
        left = [zero] + [pltpu.roll(v[t, c], 1, 1) for c in range(ncol)]
        right = [pltpu.roll(v[t, c], LANES - 1, 1) for c in range(ncol)] + [zero]
        for c in range(ncol):
            a = up[t, c] if t == 0 else jnp.where(row == 0, up[t - 1, c], up[t, c])
            b = down[t, c] if t == top - 1 else jnp.where(row == 7, down[t + 1, c], down[t, c])
            l = jnp.where(lane == 0, left[c], left[c + 1])
            r = jnp.where(lane == LANES - 1, right[c + 1], right[c])
            where = tile(t, c)
            total = (ref[(x - 1, *where)] + ref[(x + 1, *where)]) + (a + b) + (l + r)
            yield t, c, v[t, c], total


def tile(t, c):
    return slice(8 * t, 8 * t + 8), slice(LANES * c, LANES * c + LANES)


def edges():
    ix, iy = lax.axis_index("px"), lax.axis_index("py")
    nx, ny = lax.axis_size("px"), lax.axis_size("py")
    flag = lambda cond: jnp.where(cond, 0.0, 1.0).astype(F32)
    return flag(ix == 0), flag(ix == nx - 1), flag(iy == 0), flag(iy == ny - 1)


def krylov(u_ref, w_refs, lo, hi, known_ref, sums_ref):
    planes, top, ncol = u_ref.shape[0], u_ref.shape[1] // 8, u_ref.shape[2] // LANES
    x_lo, x_hi, y_lo, y_hi = edges()
    first, last = HX, planes - HX

    def mask(x, t):
        along = x_lo if x < first else x_hi if x >= last else None
        across = y_lo if t == 0 else y_hi if t == top - 1 else None
        if along is None or across is None:
            return across if along is None else along
        return along * across

    for k in range(ITERS):
        src, dst = u_ref if k == 0 else w_refs[k - 1], w_refs[k]
        for x in range(lo + k, hi - k):
            for t, c, v, total in plane_sums(src, x, range(top)):
                if k == 0:
                    value = total - v * (4.0 + 2.0 * (v * v))
                else:
                    u = u_ref[(x, *tile(t, c))]
                    value = total + (2.0 - 6.0 * (u * u)) * v
                m = mask(x, t)
                dst[(x, *tile(t, c))] = value if m is None else value * m
    own = range(HY // 8, top - HY // 8)
    zero = jnp.zeros((8, LANES), F32)
    mus = [zero] * 8
    more = [zero] * (KNOWN * (ITERS + 1))
    for x in range(first, last):
        for t, c, w2, total in plane_sums(w_refs[2], x, own):
            u, w0, w1 = (ref[(x, *tile(t, c))] for ref in (u_ref, w_refs[0], w_refs[1]))
            w3 = total + (2.0 - 6.0 * (u * u)) * w2
            pairs = ((w0, w0), (w0, w1), (w1, w1), (w1, w2), (w2, w2), (w2, w3), (w3, w3))
            for n, (p, q) in enumerate(pairs):
                mus[n] = mus[n] + p * q
    for x in range(first, last):
        for t in own:
            for c in range(ncol):
                u, *ws = (ref[(x, *tile(t, c))] for ref in (u_ref, *w_refs))
                for i in range(KNOWN):
                    d = u - known_ref[(i, x - first, *tile(t - HY // 8, c))]
                    more[i] = more[i] + d * d
                    for m in range(ITERS):
                        n = KNOWN * (m + 1) + i
                        more[n] = more[n] + d * ws[m]
    block = jnp.concatenate([jnp.sum(a, axis=0, keepdims=True) for a in (*mus, *more)], axis=0)
    totals = jnp.sum(block, axis=1, keepdims=True)
    hit = lax.broadcasted_iota(jnp.int32, block.shape, 0) == lax.broadcasted_iota(jnp.int32, block.shape, 1)
    line = jnp.sum(jnp.where(hit, totals, 0.0), axis=0, keepdims=True)
    sums_ref[...] = jnp.broadcast_to(line, sums_ref.shape)


def coefficients(recv_ref, cells):
    line = jnp.sum(recv_ref[...], axis=0, keepdims=True)
    line = jnp.broadcast_to(line, (8, LANES))
    mu = [jnp.broadcast_to(line[:, n:n + 1], (8, LANES)) for n in range(7)]
    zero = jnp.zeros((8, LANES), F32)

    def inner(p, q):
        total = None
        for i, a in enumerate(p):
            if a is None:
                continue
            part = None
            for j, b in enumerate(q):
                if b is None:
                    continue
                term = b * mu[i + j]
                part = term if part is None else part + term
            part = a * part
            total = part if total is None else total + part
        return total

    beta = jnp.sqrt(0.25 * mu[0] + EPS)
    basis = [[-0.5 / beta]]
    hess = {}
    for k in range(ITERS):
        vec = basis[k]
        image = [None] * (k + 2)
        for i in range(k + 2):
            a = 0.5 * vec[i - 1] if i > 0 else None
            b = -3.0 * vec[i] if i <= k else None
            image[i] = b if a is None else (a if b is None else a + b)
        for j in range(k + 1):
            hess[j, k] = inner(basis[j], image)
        rest = list(image)
        for j in range(k + 1):
            for i in range(len(basis[j])):
                rest[i] = rest[i] - hess[j, k] * basis[j][i]
        square = jnp.maximum(inner(rest, rest), 0.0)
        hess[k + 1, k] = jnp.sqrt(square + EPS)
        if k < ITERS - 1:
            scale = 1.0 / hess[k + 1, k]
            basis.append([a * scale for a in rest])

    def normal(i, j):
        total = None
        for r in range(ITERS + 1):
            if (r, i) in hess and (r, j) in hess:
                term = hess[r, i] * hess[r, j]
                total = term if total is None else total + term
        return total

    lower = {}
    for j in range(ITERS):
        diag = normal(j, j)
        for r in range(j):
            diag = diag - lower[j, r] * lower[j, r]
        lower[j, j] = jnp.sqrt(diag)
        for i in range(j + 1, ITERS):
            off = normal(i, j)
            for r in range(j):
                off = off - lower[i, r] * lower[j, r]
            lower[i, j] = off / lower[j, j]
    forward = []
    for i in range(ITERS):
        part = beta * hess[0, i]
        for j in range(i):
            part = part - lower[i, j] * forward[j]
        forward.append(part / lower[i, i])
    back = [None] * ITERS
    for i in reversed(range(ITERS)):
        part = forward[i]
        for j in range(i + 1, ITERS):
            part = part - lower[j, i] * back[j]
        back[i] = part / lower[i, i]
    coef = []
    for m in range(ITERS):
        total = zero
        for j in range(m, ITERS):
            total = total + back[j] * basis[j][m]
        coef.append(total)
    lane = lax.broadcasted_iota(jnp.int32, (8, LANES), 1)
    dist = pltpu.roll(line, LANES - DIST, 1)
    dot = zero
    for m in range(ITERS):
        dot = dot + coef[m] * pltpu.roll(line, LANES - CROSS - KNOWN * m, 1)
    mean = dist / cells + EPS
    weight = 1.0 / mean + DEFLATE
    terms = jnp.where(lane < KNOWN, 2.0 * dot / (cells * mean * mean * weight), 0.0)
    total = jnp.sum(terms, axis=1, keepdims=True)
    tau = 1.0 / (1.0 + jnp.abs(jnp.broadcast_to(total, (8, LANES))))
    return [tau * a for a in coef]


def update(u_ref, w_refs, coef, dst, lo, hi):
    top, ncol = u_ref.shape[1] // 8, u_ref.shape[2] // LANES
    for x in range(lo, hi):
        for t in range(top):
            for c in range(ncol):
                where = (x, *tile(t, c))
                value = u_ref[where]
                for a, w in zip(coef, w_refs):
                    value = value + a * w[where]
                dst[where] = value


def parity(axis):
    return lax.axis_index(axis) % 2


def load_kernel(field_hbm, known_hbm, field_ref, known_ref, sems):
    pairs = ((field_hbm, field_ref), (known_hbm, known_ref))
    copies = [pltpu.make_async_copy(a, b, sems.at[n]) for n, (a, b) in enumerate(pairs)]
    for copy in copies:
        copy.start()
    for copy in copies:
        copy.wait()


def join_kernel(own_ref, first_ref, second_ref, mid_ref, up_ref, down_ref):
    bx, by, bz = own_ref.shape
    odd = parity("px")
    mid_ref[pl.ds((1 - odd) * (HX + bx), HX)] = first_ref[pl.ds(odd * (bx - HX), HX)]
    mid_ref[pl.ds(odd * (HX + bx), HX)] = second_ref[pl.ds((1 - odd) * (bx - HX), HX)]
    mid_ref[HX:HX + bx] = own_ref[...]
    odd = parity("py")
    count = up_ref.shape[0]
    high = pl.multiple_of((1 - odd) * (by - HY), HY)
    low = pl.multiple_of(odd * (by - HY), HY)
    up_ref[...] = mid_ref[1:1 + count, pl.ds(high, HY)]
    down_ref[...] = mid_ref[1:1 + count, pl.ds(low, HY)]


def first_kernel(mid_ref, up_ref, down_ref, known_ref, u_ref, w0, w1, w2, sums_ref):
    planes, rows, bz = u_ref.shape
    by = rows - 2 * HY
    count = up_ref.shape[0]
    odd = parity("py")
    edge = jnp.zeros((1, HY, bz), F32)
    for x in (0, planes - 1):
        for y in (0, HY + by):
            u_ref[x:x + 1, y:y + HY] = edge
    u_ref[:, HY:HY + by] = mid_ref[...]
    high = pl.multiple_of((1 - odd) * (HY + by), HY)
    low = pl.multiple_of(odd * (HY + by), HY)
    u_ref[1:1 + count, pl.ds(high, HY)] = up_ref[...]
    u_ref[1:1 + count, pl.ds(low, HY)] = down_ref[...]
    krylov(u_ref, (w0, w1, w2), 1, planes - 1, known_ref, sums_ref)


def second_kernel(cells, recv_ref, u_ref, a0, a1, a2, known_ref, v_ref, w0, w1, w2, sums_ref):
    coef = coefficients(recv_ref, cells)
    planes = u_ref.shape[0]
    update(u_ref, (a0, a1, a2), coef, v_ref, 3, planes - 3)
    krylov(v_ref, (w0, w1, w2), 4, planes - 4, known_ref, sums_ref)


def third_kernel(cells, recv_ref, u_ref, a0, a1, a2, out_ref, res_ref, v_ref):
    coef = coefficients(recv_ref, cells)
    planes, top = u_ref.shape[0], u_ref.shape[1] // 8
    update(u_ref, (a0, a1, a2), coef, v_ref, HX - 1, planes - HX + 1)
    for x in range(HX, planes - HX):
        for t, c, v, total in plane_sums(v_ref, x, range(HY // 8, top - HY // 8)):
            where = (x - HX, *tile(t - HY // 8, c))
            out_ref[where] = v
            res_ref[where] = 0.5 * total - v * (2.0 + v * v)


def total_over_devices(rows):
    count = rows.shape[0]
    rows = rows.reshape(count, 1, LANES)
    return lax.all_to_all(rows, AXES, 0, 0).reshape(count, LANES)


def swap(part, axis, first):
    pairs = []
    for i in range(first, lax.axis_size(axis) - 1, 2):
        pairs += [(i, i + 1), (i + 1, i)]
    return lax.ppermute(part, axis, pairs)


def local(start_field, known):
    bx, by, bz = start_field.shape
    devices = lax.axis_size("px") * lax.axis_size("py")
    cells = float(bx * by * bz * devices)
    vmem = pl.BlockSpec(memory_space=pltpu.VMEM)
    params = pltpu.CompilerParams(vmem_limit_bytes=24 * 2**20)
    shape = lambda *dims: jax.ShapeDtypeStruct(dims, F32)

    def call(body, name, outs, *args, scratch=(), space=pltpu.VMEM):
        return pl.pallas_call(
            body,
            out_shape=outs,
            in_specs=[pl.BlockSpec(memory_space=space)] * len(args),
            out_specs=tuple(vmem for _ in outs),
            scratch_shapes=scratch,
            compiler_params=params,
            name=name,
        )(*args)

    planes, rows = bx + 2 * HX, by + 2 * HY
    first, second = swap(start_field, "px", 0), swap(start_field, "px", 1)
    own = shape(bx, by, bz)
    sems = [pltpu.SemaphoreType.DMA((2,))]
    loaded = (own, shape(*known.shape))
    mine, known = call(load_kernel, "load", loaded, start_field, known, scratch=sems, space=pltpu.HBM)
    strip = shape(planes - 2, HY, bz)
    mid, up, down = call(join_kernel, "join", (shape(planes, by, bz), strip, strip), mine, first, second)
    up, down = swap(up, "py", 0), swap(down, "py", 1)
    whole = shape(planes, rows, bz)
    sums = shape(devices, LANES)
    u, a0, a1, a2, sent = call(first_kernel, "first_step", (whole,) * 4 + (sums,), mid, up, down, known)
    recv = total_over_devices(sent)
    body = lambda *refs: second_kernel(cells, *refs)
    v, b0, b1, b2, sent = call(body, "second_step", (whole,) * 4 + (sums,), recv, u, a0, a1, a2, known)
    recv = total_over_devices(sent)
    body = lambda *refs: third_kernel(cells, *refs)
    scratch = [pltpu.VMEM(whole.shape, F32)]
    field, residual = call(body, "finish", (own, own), recv, v, b0, b1, b2, scratch=scratch)
    return field, residual


def solution(mesh):
    placed = (P("px", "py", None), P(None, "px", "py", None))
    return jax.shard_map(
        local,
        mesh=mesh,
        in_specs=placed,
        out_specs=(P("px", "py", None), P("px", "py", None)),
        check_vma=False,
    )
```

time: 84.5 us -> 77.2 us (0.914)
  Pallas kernels: 16.2 us -> 7.81 us
  blocking collectives: 50.6 us -> 47.5 us
  waiting for transfers between devices: 5.08 us -> 8.11 us
  starting transfers between devices: 9.14 us -> 10.3 us
    pallas_call x6 -> x5, Pallas kernels: 16.2 us -> 7.81 us  [call(): pl.pallas_call(body, out_shape=outs, in_specs=[pl.BlockSpec(memory_space=...]
    all_to_all x2, blocking collectives: 50.6 us -> 47.5 us  [total_over_devices(): return lax.all_to_all(rows, AXES, 0, 0).reshape(count, LANES)]
    ppermute x4, waiting for transfers between devices: 5.08 us -> 8.11 us  [swap(): return lax.ppermute(part, axis, pairs)]
    ppermute x4, starting transfers between devices: 9.14 us -> 10.3 us  [swap(): return lax.ppermute(part, axis, pairs)]
  transfers between devices with their start and end apart: 4 -> 4, of which waited for: 2 -> 2; matrix products, arithmetic and copies ran while one was open for 0% -> 0% of each run, Pallas kernels for 2% -> 0%
where the time goes in v3:
time: 77.2 us; the launch traced here: 77 us
  blocking collectives  47.5 us (62%)
  starting transfers between devices  10.3 us (13%)
  waiting for transfers between devices  8.11 us (11%)
  Pallas kernels  7.81 us (10%)
  local copies, waits for them, and re-layouts  2.54 us (3%)
    all_to_all x2, blocking collectives, total_over_devices(): return lax.all_to_all(rows, AXES, 0, 0).reshape(count, LANES)  47.5 us
    ppermute x4, starting transfers between devices, swap(): return lax.ppermute(part, axis, pairs)  10.3 us
    ppermute x4, waiting for transfers between devices, swap(): return lax.ppermute(part, axis, pairs)  8.11 us
    pallas_call x5, Pallas kernels, call(): pl.pallas_call(body, out_shape=outs, in_specs=[pl.BlockSpec(memory_space=...  7.81 us
    unnamed x4, local copies, waits for them, and re-layouts  2.54 us
  transfers between devices with their start and end apart: 4, of which 2 were waited for; matrix products, arithmetic and copies ran while one was open for 0% of the time, Pallas kernels for 0%

profile of v3, /device:TPU:1, one launch (start us, length us, event | category | flops | bytes accessed | tf_op | source)
XLA Modules:
  0.0 77.0 jit_solution(3950917738509671161)
XLA Ops:
  0.6 0.7 collective-permute-start.1
  1.3 4.6 %collective-permute-start = (f32[8,16,512]{2,1,0:T(8,128)}, f32[8,16,512]{2,1,0:T(8,128)S(1)}, u32[]{:S(2)}, u32[]{:S(2)}) collective-permute-start(f32[8,16,512]{2,1,0:T(8,128)} %field_hbm.1), channel_id=1, source_target_pairs={{0,16},{16,0},{32,48},{48,32},{64,80},{80,64},{96,112},{112,96},{1... | collective-permute-start | bytes 786440 | tf_op jit(solution)/shard_map/ppermute | solution.py:287
  5.9 0.0 copy-start
  5.9 1.6 %copy-done = f32[8,8,16,512]{3,2,1,0:T(8,128)S(1)} copy-done((f32[8,8,16,512]{3,2,1,0:T(8,128)S(1)}, f32[8,8,16,512]{3,2,1,0:T(8,128)}, u32[]{:S(2)}) %copy-start) | copy-done | bytes 2097176
  7.5 0.0 copy-start.1
  7.5 0.9 %copy-done.1 = f32[8,16,512]{2,1,0:T(8,128)S(1)} copy-done((f32[8,16,512]{2,1,0:T(8,128)S(1)}, f32[8,16,512]{2,1,0:T(8,128)}, u32[]{:S(2)}) %copy-start.1) | copy-done | bytes 262168
  8.4 0.2 load.1
  8.6 0.0 collective-permute-done.1.second_ref
  8.6 3.2 %collective-permute-done.first_ref = f32[8,16,512]{2,1,0:T(8,128)S(1)} collective-permute-done((f32[8,16,512]{2,1,0:T(8,128)}, f32[8,16,512]{2,1,0:T(8,128)S(1)}, u32[]{:S(2)}, u32[]{:S(2)}) %collective-permute-start) | collective-permute-done | bytes 262176 | tf_op jit(solution)/shard_map/ppermute | solution.py:287
  11.8 0.1 join.1
  11.9 1.6 %collective-permute-start.2 = (f32[20,8,512]{2,1,0:T(8,128)S(1)}, f32[20,8,512]{2,1,0:T(8,128)S(1)}, u32[]{:S(2)}, u32[]{:S(2)}) collective-permute-start(f32[20,8,512]{2,1,0:T(8,128)S(1)} %get-tuple-element.19), channel_id=1, source_target_pairs={{0,1},{1,0},{2,3},{3,2},{4,5},{5,4},{6,7},{7,6},{8,9},{9,8},{10,11... | collective-permute-start | bytes 983048 | tf_op jit(solution)/shard_map/ppermute | solution.py:287
  13.5 3.4 %collective-permute-start.3 = (f32[20,8,512]{2,1,0:T(8,128)S(1)}, f32[20,8,512]{2,1,0:T(8,128)S(1)}, u32[]{:S(2)}, u32[]{:S(2)}) collective-permute-start(f32[20,8,512]{2,1,0:T(8,128)S(1)} %get-tuple-element.20), channel_id=1, source_target_pairs={{1,2},{2,1},{3,4},{4,3},{5,6},{6,5},{7,8},{8,7},{9,10},{10,9},{11,... | collective-permute-start | bytes 983048 | tf_op jit(solution)/shard_map/ppermute | solution.py:287
  17.0 0.0 collective-permute-done.2.up_ref
  17.0 4.9 %collective-permute-done.3.down_ref = f32[20,8,512]{2,1,0:T(8,128)S(1)} collective-permute-done((f32[20,8,512]{2,1,0:T(8,128)S(1)}, f32[20,8,512]{2,1,0:T(8,128)S(1)}, u32[]{:S(2)}, u32[]{:S(2)}) %collective-permute-start.3) | collective-permute-done | bytes 327712 | tf_op jit(solution)/shard_map/ppermute | solution.py:287
  21.9 3.3 %first_step.1 = (f32[22,32,512]{2,1,0:T(8,128)S(1)}, f32[22,32,512]{2,1,0:T(8,128)S(1)}, f32[22,32,512]{2,1,0:T(8,128)S(1)}, f32[22,32,512]{2,1,0:T(8,128)S(1)}, f32[256,128]{1,0:T(8,128)S(1)}) custom-call(f32[22,16,512]{2,1,0:T(8,128)S(1)} %get-tuple-element.18.mid_ref, f32[20,8,512]{2,1,0:T(8,128)S(1)} %collective-permute-done.2.up_ref, ...), custom_call_target="tpu_custom_call" | custom-call | tf_op jit(solution)/shard_map/first_step/pallas_call | solution.py:299
  25.2 28.9 %all_to_all.10 = f32[256,1,128]{2,1,0:T(1,128)S(1)} all-to-all(f32[256,1,128]{2,1,0:T(1,128)S(1)} %bitcast.11), channel_id=1, replica_groups=mesh['px'=16,'py'=16] {'px','py'}, dimensions={0} | all-to-all | bytes 262144 | tf_op jit(solution)/shard_map/all_to_all | solution.py:280
  54.1 2.9 %second_step.1 = (f32[22,32,512]{2,1,0:T(8,128)S(1)}, f32[22,32,512]{2,1,0:T(8,128)S(1)}, f32[22,32,512]{2,1,0:T(8,128)S(1)}, f32[22,32,512]{2,1,0:T(8,128)S(1)}, f32[256,128]{1,0:T(8,128)S(1)}) custom-call(f32[256,128]{1,0:T(8,128)S(1)} %bitcast.8, f32[22,32,512]{2,1,0:T(8,128)S(1)} %get-tuple-element.23.refs_1_, ...), custom_call_target="tpu_custom_call" | custom-call | tf_op jit(solution)/shard_map/second_step/pallas_call | solution.py:299
  57.0 18.6 %all_to_all.11 = f32[256,1,128]{2,1,0:T(1,128)S(1)} all-to-all(f32[256,1,128]{2,1,0:T(1,128)S(1)} %bitcast.10), channel_id=1, replica_groups=mesh['px'=16,'py'=16] {'px','py'}, dimensions={0} | all-to-all | bytes 262144 | tf_op jit(solution)/shard_map/all_to_all | solution.py:280
  75.7 1.3 %finish.1 = (f32[8,16,512]{2,1,0:T(8,128)}, f32[8,16,512]{2,1,0:T(8,128)}) custom-call(f32[256,128]{1,0:T(8,128)S(1)} %bitcast.9, f32[22,32,512]{2,1,0:T(8,128)S(1)} %get-tuple-element.28.refs_1_, f32[22,32,512]{2,1,0:T(8,128)S(1)} %get-tuple-element.29.refs_2_, f32[22,32,512]{2,1,0:T(8,128)S(1)} %get-tuple-element.30.refs_3_, ...), custom_call_target="tpu_custom_call" | custom-call | tf_op jit(solution)/shard_map/finish/pallas_call | solution.py:299
Async XLA Ops:
  0.6 8.0 %collective-permute-start.1 = (f32[8,16,512]{2,1,0:T(8,128)}, f32[8,16,512]{2,1,0:T(8,128)S(1)}, u32[]{:S(2)}, u32[]{:S(2)}) collective-permute-start(f32[8,16,512]{2,1,0:T(8,128)} %field_hbm.1), channel_id=1, source_target_pairs={{16,32},{32,16},{48,64},{64,48},{80,96},{96,80},{112,128},{128,112... | collective-permute-start | bytes 786440 | tf_op jit(solution)/shard_map/ppermute | solution.py:287
  1.3 10.5 %collective-permute-start = (f32[8,16,512]{2,1,0:T(8,128)}, f32[8,16,512]{2,1,0:T(8,128)S(1)}, u32[]{:S(2)}, u32[]{:S(2)}) collective-permute-start(f32[8,16,512]{2,1,0:T(8,128)} %field_hbm.1), channel_id=1, source_target_pairs={{0,16},{16,0},{32,48},{48,32},{64,80},{80,64},{96,112},{112,96},{1... | collective-permute-start | bytes 786440 | tf_op jit(solution)/shard_map/ppermute | solution.py:287
  5.9 1.6 %copy-start = (f32[8,8,16,512]{3,2,1,0:T(8,128)S(1)}, f32[8,8,16,512]{3,2,1,0:T(8,128)}, u32[]{:S(2)}) copy-start(f32[8,8,16,512]{3,2,1,0:T(8,128)} %known_hbm.1) | copy-start | bytes 6291460
  7.5 0.9 %copy-start.1 = (f32[8,16,512]{2,1,0:T(8,128)S(1)}, f32[8,16,512]{2,1,0:T(8,128)}, u32[]{:S(2)}) copy-start(f32[8,16,512]{2,1,0:T(8,128)} %field_hbm.1) | copy-start | bytes 786436
  11.9 5.1 %collective-permute-start.2 = (f32[20,8,512]{2,1,0:T(8,128)S(1)}, f32[20,8,512]{2,1,0:T(8,128)S(1)}, u32[]{:S(2)}, u32[]{:S(2)}) collective-permute-start(f32[20,8,512]{2,1,0:T(8,128)S(1)} %get-tuple-element.19), channel_id=1, source_target_pairs={{0,1},{1,0},{2,3},{3,2},{4,5},{5,4},{6,7},{7,6},{8,9},{9,8},{10,11... | collective-permute-start | bytes 983048 | tf_op jit(solution)/shard_map/ppermute | solution.py:287
  13.5 8.4 %collective-permute-start.3 = (f32[20,8,512]{2,1,0:T(8,128)S(1)}, f32[20,8,512]{2,1,0:T(8,128)S(1)}, u32[]{:S(2)}, u32[]{:S(2)}) collective-permute-start(f32[20,8,512]{2,1,0:T(8,128)S(1)} %get-tuple-element.20), channel_id=1, source_target_pairs={{1,2},{2,1},{3,4},{4,3},{5,6},{6,5},{7,8},{8,7},{9,10},{10,9},{11,... | collective-permute-start | bytes 983048 | tf_op jit(solution)/shard_map/ppermute | solution.py:287

commit v4 on v3

--- a/solution.py
+++ b/solution.py
@@ -56,7 +56,7 @@
     return flag(ix == 0), flag(ix == nx - 1), flag(iy == 0), flag(iy == ny - 1)
 
 
-def krylov(u_ref, w_refs, lo, hi, known_ref, sums_ref):
+def krylov(u_ref, w_refs, lo, hi, known_ref, gap, sums_ref):
     planes, top, ncol = u_ref.shape[0], u_ref.shape[1] // 8, u_ref.shape[2] // LANES
     x_lo, x_hi, y_lo, y_hi = edges()
     first, last = HX, planes - HX
@@ -83,6 +83,8 @@
     zero = jnp.zeros((8, LANES), F32)
     mus = [zero] * 8
     more = [zero] * (KNOWN * (ITERS + 1))
+    if gap is not None:
+        more[:KNOWN] = [gap[1][i] for i in range(KNOWN)]
     for x in range(first, last):
         for t, c, w2, total in plane_sums(w_refs[2], x, own):
             u, w0, w1 = (ref[(x, *tile(t, c))] for ref in (u_ref, w_refs[0], w_refs[1]))
@@ -95,8 +97,12 @@
             for c in range(ncol):
                 u, *ws = (ref[(x, *tile(t, c))] for ref in (u_ref, *w_refs))
                 for i in range(KNOWN):
-                    d = u - known_ref[(i, x - first, *tile(t - HY // 8, c))]
-                    more[i] = more[i] + d * d
+                    where = (i, x - first, *tile(t - HY // 8, c))
+                    if gap is None:
+                        d = u - known_ref[where]
+                        more[i] = more[i] + d * d
+                    else:
+                        d = gap[0][where]
                     for m in range(ITERS):
                         n = KNOWN * (m + 1) + i
                         more[n] = more[n] + d * ws[m]
@@ -216,30 +222,66 @@
     return lax.axis_index(axis) % 2
 
 
-def load_kernel(field_hbm, known_hbm, field_ref, known_ref, sems):
-    pairs = ((field_hbm, field_ref), (known_hbm, known_ref))
-    copies = [pltpu.make_async_copy(a, b, sems.at[n]) for n, (a, b) in enumerate(pairs)]
-    for copy in copies:
-        copy.start()
-    for copy in copies:
-        copy.wait()
-
-
-def join_kernel(own_ref, first_ref, second_ref, mid_ref, up_ref, down_ref):
+def edge_kernel(field_ref, rows_ref):
+    by = field_ref.shape[1]
+    start = pl.multiple_of(parity("py") * (by - HY), HY)
+    rows_ref[...] = field_ref[:, pl.ds(start, HY)]
+
+
+def gap_kernel(field_ref, known_ref, out_ref, gap_ref, dist_ref):
+    count, bx, by, bz = known_ref.shape
+    for i in range(count):
+        total = None
+        for x in range(bx):
+            for t in range(by // 8):
+                for c in range(bz // LANES):
+                    where = tile(t, c)
+                    k = known_ref[(i, x, *where)]
+                    d = field_ref[(x, *where)] - k
+                    out_ref[(i, x, *where)] = k
+                    gap_ref[(i, x, *where)] = d
+                    total = d * d if total is None else total + d * d
+        dist_ref[i] = total
+
+
+def strip_planes(planes):
+    last = planes - 1
+    full = (5, 6, last - 6, last - 5)
+    pairs = ((1, 2), (3, 4), (last - 4, last - 3), (last - 2, last - 1))
+    return full, pairs
+
+
+def half_turn(value, flag):
+    return jnp.where(flag, pltpu.roll(value, 4, 0), value)
+
+
+def join_kernel(own_ref, first_ref, second_ref, rows_ref, u_ref, up_ref, strip_ref):
     bx, by, bz = own_ref.shape
+    planes = u_ref.shape[0]
+    mine = slice(HY, HY + by)
     odd = parity("px")
-    mid_ref[pl.ds((1 - odd) * (HX + bx), HX)] = first_ref[pl.ds(odd * (bx - HX), HX)]
-    mid_ref[pl.ds(odd * (HX + bx), HX)] = second_ref[pl.ds((1 - odd) * (bx - HX), HX)]
-    mid_ref[HX:HX + bx] = own_ref[...]
+    u_ref[pl.ds((1 - odd) * (HX + bx), HX), mine] = first_ref[pl.ds(odd * (bx - HX), HX)]
+    u_ref[pl.ds(odd * (HX + bx), HX), mine] = second_ref[pl.ds((1 - odd) * (bx - HX), HX)]
+    u_ref[HX:HX + bx, mine] = own_ref[...]
     odd = parity("py")
+    u_ref[HX:HX + bx, pl.ds(pl.multiple_of(odd * (HY + by), HY), HY)] = rows_ref[...]
     count = up_ref.shape[0]
-    high = pl.multiple_of((1 - odd) * (by - HY), HY)
-    low = pl.multiple_of(odd * (by - HY), HY)
-    up_ref[...] = mid_ref[1:1 + count, pl.ds(high, HY)]
-    down_ref[...] = mid_ref[1:1 + count, pl.ds(low, HY)]
-
-
-def first_kernel(mid_ref, up_ref, down_ref, known_ref, u_ref, w0, w1, w2, sums_ref):
+    high = pl.multiple_of(HY + (1 - odd) * (by - HY), HY)
+    low = pl.multiple_of(HY + odd * (by - HY), HY)
+    up_ref[...] = u_ref[1:1 + count, pl.ds(high, HY)]
+    row, _ = iotas()
+    full, pairs = strip_planes(planes)
+    for n, x in enumerate(full):
+        strip_ref[n] = u_ref[x, pl.ds(low, HY)]
+    for n, (x, y) in enumerate(pairs):
+        for c in range(bz // LANES):
+            cols = slice(LANES * c, LANES * c + LANES)
+            a = half_turn(u_ref[x, pl.ds(low, HY), cols], odd == 1)
+            b = half_turn(u_ref[y, pl.ds(low, HY), cols], odd == 0)
+            strip_ref[len(full) + n, :, cols] = jnp.where(row < 4, a, b)
+
+
+def first_kernel(mid_ref, up_ref, strip_ref, gap_ref, dist_ref, u_ref, w0, w1, w2, sums_ref):
     planes, rows, bz = u_ref.shape
     by = rows - 2 * HY
     count = up_ref.shape[0]
@@ -248,19 +290,26 @@
     for x in (0, planes - 1):
         for y in (0, HY + by):
             u_ref[x:x + 1, y:y + HY] = edge
-    u_ref[:, HY:HY + by] = mid_ref[...]
     high = pl.multiple_of((1 - odd) * (HY + by), HY)
     low = pl.multiple_of(odd * (HY + by), HY)
     u_ref[1:1 + count, pl.ds(high, HY)] = up_ref[...]
-    u_ref[1:1 + count, pl.ds(low, HY)] = down_ref[...]
-    krylov(u_ref, (w0, w1, w2), 1, planes - 1, known_ref, sums_ref)
+    full, pairs = strip_planes(planes)
+    for n, x in enumerate(full):
+        u_ref[x, pl.ds(low, HY)] = strip_ref[n]
+    for n, (x, y) in enumerate(pairs):
+        for c in range(bz // LANES):
+            cols = slice(LANES * c, LANES * c + LANES)
+            both = strip_ref[len(full) + n, :, cols]
+            u_ref[x, pl.ds(low, HY), cols] = half_turn(both, odd == 0)
+            u_ref[y, pl.ds(low, HY), cols] = half_turn(both, odd == 1)
+    krylov(u_ref, (w0, w1, w2), 1, planes - 1, None, (gap_ref, dist_ref), sums_ref)
 
 
 def second_kernel(cells, recv_ref, u_ref, a0, a1, a2, known_ref, v_ref, w0, w1, w2, sums_ref):
     coef = coefficients(recv_ref, cells)
     planes = u_ref.shape[0]
     update(u_ref, (a0, a1, a2), coef, v_ref, 3, planes - 3)
-    krylov(v_ref, (w0, w1, w2), 4, planes - 4, known_ref, sums_ref)
+    krylov(v_ref, (w0, w1, w2), 4, planes - 4, known_ref, None, sums_ref)
 
 
 def third_kernel(cells, recv_ref, u_ref, a0, a1, a2, out_ref, res_ref, v_ref):
@@ -295,32 +344,35 @@
     params = pltpu.CompilerParams(vmem_limit_bytes=24 * 2**20)
     shape = lambda *dims: jax.ShapeDtypeStruct(dims, F32)
 
-    def call(body, name, outs, *args, scratch=(), space=pltpu.VMEM):
+    def call(body, name, outs, *args, scratch=(), alias={}):
         return pl.pallas_call(
             body,
             out_shape=outs,
-            in_specs=[pl.BlockSpec(memory_space=space)] * len(args),
+            in_specs=[vmem] * len(args),
             out_specs=tuple(vmem for _ in outs),
             scratch_shapes=scratch,
+            input_output_aliases=alias,
             compiler_params=params,
             name=name,
         )(*args)
 
     planes, rows = bx + 2 * HX, by + 2 * HY
+    own, whole = shape(bx, by, bz), shape(planes, rows, bz)
+    sums = shape(devices, LANES)
     first, second = swap(start_field, "px", 0), swap(start_field, "px", 1)
-    own = shape(bx, by, bz)
-    sems = [pltpu.SemaphoreType.DMA((2,))]
-    loaded = (own, shape(*known.shape))
-    mine, known = call(load_kernel, "load", loaded, start_field, known, scratch=sems, space=pltpu.HBM)
-    strip = shape(planes - 2, HY, bz)
-    mid, up, down = call(join_kernel, "join", (shape(planes, by, bz), strip, strip), mine, first, second)
-    up, down = swap(up, "py", 0), swap(down, "py", 1)
-    whole = shape(planes, rows, bz)
-    sums = shape(devices, LANES)
-    u, a0, a1, a2, sent = call(first_kernel, "first_step", (whole,) * 4 + (sums,), mid, up, down, known)
+    (edge,) = call(edge_kernel, "edge", (shape(bx, HY, bz),), start_field)
+    edge = swap(edge, "py", 1)
+    full, pairs = strip_planes(planes)
+    parts = (whole, shape(planes - 2, HY, bz), shape(len(full) + len(pairs), HY, bz))
+    u, up, strip = call(join_kernel, "join", parts, start_field, first, second, edge)
+    up, strip = swap(up, "py", 0), swap(strip, "py", 1)
+    parts = (shape(*known.shape), shape(*known.shape), shape(KNOWN, 8, LANES))
+    known, gap, dist = call(gap_kernel, "gap", parts, start_field, known)
+    step = (whole,) * 4 + (sums,)
+    u, a0, a1, a2, sent = call(first_kernel, "first_step", step, u, up, strip, gap, dist, alias={0: 0})
     recv = total_over_devices(sent)
     body = lambda *refs: second_kernel(cells, *refs)
-    v, b0, b1, b2, sent = call(body, "second_step", (whole,) * 4 + (sums,), recv, u, a0, a1, a2, known)
+    v, b0, b1, b2, sent = call(body, "second_step", step, recv, u, a0, a1, a2, known)
     recv = total_over_devices(sent)
     body = lambda *refs: third_kernel(cells, *refs)
     scratch = [pltpu.VMEM(whole.shape, F32)]

time: 77.2 us -> 75.8 us (0.982)
  waiting for transfers between devices: 8.11 us -> 3.25 us
  starting transfers between devices: 10.3 us -> 13.9 us
    ppermute x4 -> x5, waiting for transfers between devices: 8.11 us -> 3.25 us  [swap(): return lax.ppermute(part, axis, pairs)]
    ppermute x4 -> x5, starting transfers between devices: 10.3 us -> 13.9 us  [swap(): return lax.ppermute(part, axis, pairs)]
    pallas_call x5 -> x6, Pallas kernels: 7.81 us -> 7.81 us  [call(): pl.pallas_call(body, out_shape=outs, in_specs=[vmem] * len(args), out_spe...]
  transfers between devices with their start and end apart: 4 -> 5, of which waited for: 2 -> 2; matrix products, arithmetic and copies ran while one was open for 0% -> 0% of each run, Pallas kernels for 0% -> 1%
where the time goes in v4:
time: 75.8 us; the launch traced here: 75.5 us
  blocking collectives  47.2 us (62%)
  starting transfers between devices  13.9 us (18%)
  Pallas kernels  7.81 us (10%)
  waiting for transfers between devices  3.25 us (4%)
  local copies, waits for them, and re-layouts  2.57 us (3%)
    all_to_all x2, blocking collectives, total_over_devices(): return lax.all_to_all(rows, AXES, 0, 0).reshape(count, LANES)  47.2 us
    ppermute x5, starting transfers between devices, swap(): return lax.ppermute(part, axis, pairs)  13.9 us
    pallas_call x6, Pallas kernels, call(): pl.pallas_call(body, out_shape=outs, in_specs=[vmem] * len(args), out_spe...  7.81 us
    ppermute x5, waiting for transfers between devices, swap(): return lax.ppermute(part, axis, pairs)  3.25 us
    unnamed x4, local copies, waits for them, and re-layouts  2.57 us
  transfers between devices with their start and end apart: 5, of which 2 were waited for; matrix products, arithmetic and copies ran while one was open for 0% of the time, Pallas kernels for 1%

profile of v4, /device:TPU:1, one launch (start us, length us, event | category | flops | bytes accessed | tf_op | source)
XLA Modules:
  0.0 75.5 jit_solution(12697457151994009597)
XLA Ops:
  0.6 0.7 collective-permute-start.1
  1.3 4.6 %collective-permute-start = (f32[8,16,512]{2,1,0:T(8,128)}, f32[8,16,512]{2,1,0:T(8,128)S(1)}, u32[]{:S(2)}, u32[]{:S(2)}) collective-permute-start(f32[8,16,512]{2,1,0:T(8,128)} %field_ref.3), channel_id=1, source_target_pairs={{0,16},{16,0},{32,48},{48,32},{64,80},{80,64},{96,112},{112,96},{1... | collective-permute-start | bytes 786440 | tf_op jit(solution)/shard_map/ppermute | solution.py:336
  5.9 0.0 copy-start
  5.9 1.0 %copy-done = f32[8,16,512]{2,1,0:T(8,128)S(1)} copy-done((f32[8,16,512]{2,1,0:T(8,128)S(1)}, f32[8,16,512]{2,1,0:T(8,128)}, u32[]{:S(2)}) %copy-start) | copy-done | bytes 262168
  6.9 4.7 %collective-permute-start.2 = (f32[8,8,512]{2,1,0:T(8,128)S(1)}, f32[8,8,512]{2,1,0:T(8,128)S(1)}, u32[]{:S(2)}, u32[]{:S(2)}) collective-permute-start(f32[8,8,512]{2,1,0:T(8,128)S(1)} %edge.1), channel_id=1, source_target_pairs={{1,2},{2,1},{3,4},{4,3},{5,6},{6,5},{7,8},{8,7},{9,10},{10,9},{11,... | collective-permute-start | bytes 393224 | tf_op jit(solution)/shard_map/ppermute | solution.py:336
  11.6 2.6 %collective-permute-done.2.rows_ref = f32[8,8,512]{2,1,0:T(8,128)S(1)} collective-permute-done((f32[8,8,512]{2,1,0:T(8,128)S(1)}, f32[8,8,512]{2,1,0:T(8,128)S(1)}, u32[]{:S(2)}, u32[]{:S(2)}) %collective-permute-start.2) | collective-permute-done | bytes 131104 | tf_op jit(solution)/shard_map/ppermute | solution.py:336
  14.2 0.0 collective-permute-done.1.second_ref
  14.2 0.0 collective-permute-done.first_ref
  14.2 0.1 join.1
  14.3 0.1 collective-permute-start.3
  14.4 3.9 %collective-permute-start.4 = (f32[8,8,512]{2,1,0:T(8,128)S(1)}, f32[8,8,512]{2,1,0:T(8,128)S(1)}, u32[]{:S(2)}, u32[]{:S(2)}) collective-permute-start(f32[8,8,512]{2,1,0:T(8,128)S(1)} %get-tuple-element.20), channel_id=1, source_target_pairs={{1,2},{2,1},{3,4},{4,3},{5,6},{6,5},{7,8},{8,7},{9,10},{10,9},{11,... | collective-permute-start | bytes 393224 | tf_op jit(solution)/shard_map/ppermute | solution.py:336
  18.3 0.0 copy-start.1
  18.3 1.6 %copy-done.1 = f32[8,8,16,512]{3,2,1,0:T(8,128)S(1)} copy-done((f32[8,8,16,512]{3,2,1,0:T(8,128)S(1)}, f32[8,8,16,512]{3,2,1,0:T(8,128)}, u32[]{:S(2)}) %copy-start.1) | copy-done | bytes 2097176
  19.9 0.4 gap.1
  20.4 0.6 collective-permute-done.4.strip_ref
  21.0 0.0 collective-permute-done.3.up_ref
  21.0 3.0 %first_step.1 = (f32[22,32,512]{2,1,0:T(8,128)S(1)}, f32[22,32,512]{2,1,0:T(8,128)S(1)}, f32[22,32,512]{2,1,0:T(8,128)S(1)}, f32[22,32,512]{2,1,0:T(8,128)S(1)}, f32[256,128]{1,0:T(8,128)S(1)}) custom-call(f32[22,32,512]{2,1,0:T(8,128)S(1)} %get-tuple-element.18.mid_ref, ...), custom_call_target="tpu_custom_call", output_to_operand_aliasing={{0}: (0, {})} | custom-call | tf_op jit(solution)/shard_map/first_step/pallas_call | solution.py:348
  24.0 28.6 %all_to_all.10 = f32[256,1,128]{2,1,0:T(1,128)S(1)} all-to-all(f32[256,1,128]{2,1,0:T(1,128)S(1)} %bitcast.11), channel_id=1, replica_groups=mesh['px'=16,'py'=16] {'px','py'}, dimensions={0} | all-to-all | bytes 262144 | tf_op jit(solution)/shard_map/all_to_all | solution.py:329
  52.6 2.9 %second_step.1 = (f32[22,32,512]{2,1,0:T(8,128)S(1)}, f32[22,32,512]{2,1,0:T(8,128)S(1)}, f32[22,32,512]{2,1,0:T(8,128)S(1)}, f32[22,32,512]{2,1,0:T(8,128)S(1)}, f32[256,128]{1,0:T(8,128)S(1)}) custom-call(f32[256,128]{1,0:T(8,128)S(1)} %bitcast.8, f32[22,32,512]{2,1,0:T(8,128)S(1)} %get-tuple-element.24.refs_1_, ...), custom_call_target="tpu_custom_call" | custom-call | tf_op jit(solution)/shard_map/second_step/pallas_call | solution.py:348
  55.6 18.6 %all_to_all.11 = f32[256,1,128]{2,1,0:T(1,128)S(1)} all-to-all(f32[256,1,128]{2,1,0:T(1,128)S(1)} %bitcast.10), channel_id=1, replica_groups=mesh['px'=16,'py'=16] {'px','py'}, dimensions={0} | all-to-all | bytes 262144 | tf_op jit(solution)/shard_map/all_to_all | solution.py:329
  74.2 1.3 %finish.1 = (f32[8,16,512]{2,1,0:T(8,128)}, f32[8,16,512]{2,1,0:T(8,128)}) custom-call(f32[256,128]{1,0:T(8,128)S(1)} %bitcast.9, f32[22,32,512]{2,1,0:T(8,128)S(1)} %get-tuple-element.30.refs_1_, f32[22,32,512]{2,1,0:T(8,128)S(1)} %get-tuple-element.31.refs_2_, f32[22,32,512]{2,1,0:T(8,128)S(1)} %get-tuple-element.32.refs_3_, ...), custom_call_target="tpu_custom_call" | custom-call | tf_op jit(solution)/shard_map/finish/pallas_call | solution.py:348
  (1 shorter events, 0.0 us)
Async XLA Ops:
  0.6 13.6 %collective-permute-start.1 = (f32[8,16,512]{2,1,0:T(8,128)}, f32[8,16,512]{2,1,0:T(8,128)S(1)}, u32[]{:S(2)}, u32[]{:S(2)}) collective-permute-start(f32[8,16,512]{2,1,0:T(8,128)} %field_ref.3), channel_id=1, source_target_pairs={{16,32},{32,16},{48,64},{64,48},{80,96},{96,80},{112,128},{128,112... | collective-permute-start | bytes 786440 | tf_op jit(solution)/shard_map/ppermute | solution.py:336
  1.3 12.9 %collective-permute-start = (f32[8,16,512]{2,1,0:T(8,128)}, f32[8,16,512]{2,1,0:T(8,128)S(1)}, u32[]{:S(2)}, u32[]{:S(2)}) collective-permute-start(f32[8,16,512]{2,1,0:T(8,128)} %field_ref.3), channel_id=1, source_target_pairs={{0,16},{16,0},{32,48},{48,32},{64,80},{80,64},{96,112},{112,96},{1... | collective-permute-start | bytes 786440 | tf_op jit(solution)/shard_map/ppermute | solution.py:336
  5.9 1.0 %copy-start = (f32[8,16,512]{2,1,0:T(8,128)S(1)}, f32[8,16,512]{2,1,0:T(8,128)}, u32[]{:S(2)}) copy-start(f32[8,16,512]{2,1,0:T(8,128)} %field_ref.3) | copy-start | bytes 786436
  6.9 7.3 %collective-permute-start.2 = (f32[8,8,512]{2,1,0:T(8,128)S(1)}, f32[8,8,512]{2,1,0:T(8,128)S(1)}, u32[]{:S(2)}, u32[]{:S(2)}) collective-permute-start(f32[8,8,512]{2,1,0:T(8,128)S(1)} %edge.1), channel_id=1, source_target_pairs={{1,2},{2,1},{3,4},{4,3},{5,6},{6,5},{7,8},{8,7},{9,10},{10,9},{11,... | collective-permute-start | bytes 393224 | tf_op jit(solution)/shard_map/ppermute | solution.py:336
  14.3 6.7 %collective-permute-start.3 = (f32[20,8,512]{2,1,0:T(8,128)S(1)}, f32[20,8,512]{2,1,0:T(8,128)S(1)}, u32[]{:S(2)}, u32[]{:S(2)}) collective-permute-start(f32[20,8,512]{2,1,0:T(8,128)S(1)} %get-tuple-element.19), channel_id=1, source_target_pairs={{0,1},{1,0},{2,3},{3,2},{4,5},{5,4},{6,7},{7,6},{8,9},{9,8},{10,11... | collective-permute-start | bytes 983048 | tf_op jit(solution)/shard_map/ppermute | solution.py:336
  14.4 6.6 %collective-permute-start.4 = (f32[8,8,512]{2,1,0:T(8,128)S(1)}, f32[8,8,512]{2,1,0:T(8,128)S(1)}, u32[]{:S(2)}, u32[]{:S(2)}) collective-permute-start(f32[8,8,512]{2,1,0:T(8,128)S(1)} %get-tuple-element.20), channel_id=1, source_target_pairs={{1,2},{2,1},{3,4},{4,3},{5,6},{6,5},{7,8},{8,7},{9,10},{10,9},{11,... | collective-permute-start | bytes 393224 | tf_op jit(solution)/shard_map/ppermute | solution.py:336
  18.3 1.6 %copy-start.1 = (f32[8,8,16,512]{3,2,1,0:T(8,128)S(1)}, f32[8,8,16,512]{3,2,1,0:T(8,128)}, u32[]{:S(2)}) copy-start(f32[8,8,16,512]{3,2,1,0:T(8,128)} %known_ref.1) | copy-start | bytes 6291460

commit v5 on v4

--- a/solution.py
+++ b/solution.py
@@ -56,7 +56,7 @@
     return flag(ix == 0), flag(ix == nx - 1), flag(iy == 0), flag(iy == ny - 1)
 
 
-def krylov(u_ref, w_refs, lo, hi, known_ref, gap, sums_ref):
+def krylov(u_ref, w_refs, q_ref, lo, hi, known_ref, gap, sums_ref):
     planes, top, ncol = u_ref.shape[0], u_ref.shape[1] // 8, u_ref.shape[2] // LANES
     x_lo, x_hi, y_lo, y_hi = edges()
     first, last = HX, planes - HX
@@ -68,18 +68,21 @@
             return across if along is None else along
         return along * across
 
+    own = range(HY // 8, top - HY // 8)
     for k in range(ITERS):
         src, dst = u_ref if k == 0 else w_refs[k - 1], w_refs[k]
         for x in range(lo + k, hi - k):
-            for t, c, v, total in plane_sums(src, x, range(top)):
+            tiles = own if x in (lo + k, hi - k - 1) else range(top)
+            for t, c, v, total in plane_sums(src, x, tiles):
+                where = (x, *tile(t, c))
                 if k == 0:
-                    value = total - v * (4.0 + 2.0 * (v * v))
+                    square = v * v
+                    q_ref[where] = 2.0 - 6.0 * square
+                    value = total - v * (4.0 + 2.0 * square)
                 else:
-                    u = u_ref[(x, *tile(t, c))]
-                    value = total + (2.0 - 6.0 * (u * u)) * v
+                    value = total + q_ref[where] * v
                 m = mask(x, t)
-                dst[(x, *tile(t, c))] = value if m is None else value * m
-    own = range(HY // 8, top - HY // 8)
+                dst[where] = value if m is None else value * m
     zero = jnp.zeros((8, LANES), F32)
     mus = [zero] * 8
     more = [zero] * (KNOWN * (ITERS + 1))
@@ -87,8 +90,8 @@
         more[:KNOWN] = [gap[1][i] for i in range(KNOWN)]
     for x in range(first, last):
         for t, c, w2, total in plane_sums(w_refs[2], x, own):
-            u, w0, w1 = (ref[(x, *tile(t, c))] for ref in (u_ref, w_refs[0], w_refs[1]))
-            w3 = total + (2.0 - 6.0 * (u * u)) * w2
+            q, w0, w1 = (ref[(x, *tile(t, c))] for ref in (q_ref, w_refs[0], w_refs[1]))
+            w3 = total + q * w2
             pairs = ((w0, w0), (w0, w1), (w1, w1), (w1, w2), (w2, w2), (w2, w3), (w3, w3))
             for n, (p, q) in enumerate(pairs):
                 mus[n] = mus[n] + p * q
@@ -206,26 +209,23 @@
     return [tau * a for a in coef]
 
 
-def update(u_ref, w_refs, coef, dst, lo, hi):
+def update(u_ref, w_refs, coef, dst, lo, hi, out_ref=None):
     top, ncol = u_ref.shape[1] // 8, u_ref.shape[2] // LANES
+    own = range(HY // 8, top - HY // 8)
     for x in range(lo, hi):
-        for t in range(top):
+        for t in own if x in (lo, hi - 1) else range(top):
             for c in range(ncol):
                 where = (x, *tile(t, c))
                 value = u_ref[where]
                 for a, w in zip(coef, w_refs):
                     value = value + a * w[where]
                 dst[where] = value
+                if out_ref is not None and t in own and HX <= x < u_ref.shape[0] - HX:
+                    out_ref[(x - HX, *tile(t - HY // 8, c))] = value
 
 
 def parity(axis):
     return lax.axis_index(axis) % 2
-
-
-def edge_kernel(field_ref, rows_ref):
-    by = field_ref.shape[1]
-    start = pl.multiple_of(parity("py") * (by - HY), HY)
-    rows_ref[...] = field_ref[:, pl.ds(start, HY)]
 
 
 def gap_kernel(field_ref, known_ref, out_ref, gap_ref, dist_ref):
@@ -244,83 +244,93 @@
         dist_ref[i] = total
 
 
-def strip_planes(planes):
-    last = planes - 1
-    full = (5, 6, last - 6, last - 5)
-    pairs = ((1, 2), (3, 4), (last - 4, last - 3), (last - 2, last - 1))
-    return full, pairs
-
-
-def half_turn(value, flag):
-    return jnp.where(flag, pltpu.roll(value, 4, 0), value)
-
-
-def join_kernel(own_ref, first_ref, second_ref, rows_ref, u_ref, up_ref, strip_ref):
+SHARED = ((1, 6, 5), (2, 5, 4), (3, 4, 6))
+
+
+def shared_planes(planes):
+    for n, (d, rows, other) in enumerate(SHARED):
+        yield 2 * n, HX - d, HX - other, rows
+        yield 2 * n + 1, planes - 1 - HX + d, planes - 1 - HX + other, rows
+
+
+def pack_rows(u_ref, out_ref, high):
+    planes, rows, bz = u_ref.shape
+    bx = planes - 2 * HX
+    start = pl.multiple_of(jnp.where(high, rows - 2 * HY, HY), HY)
+    out_ref[0:bx] = u_ref[HX:HX + bx, pl.ds(start, HY)]
+    row, _ = iotas()
+    depth = jnp.where(high, HY - 1 - row, row)
+    for n, x, y, count in shared_planes(planes):
+        for c in range(bz // LANES):
+            cols = slice(LANES * c, LANES * c + LANES)
+            a, b = (u_ref[p, pl.ds(start, HY), cols] for p in (x, y))
+            b = jnp.where(high, pltpu.roll(b, HY - count, 0), pltpu.roll(b, count, 0))
+            out_ref[bx + n, :, cols] = jnp.where(depth < count, a, b)
+
+
+def unpack_rows(in_ref, u_ref, high):
+    planes, rows, bz = u_ref.shape
+    bx = planes - 2 * HX
+    start = pl.multiple_of(jnp.where(high, rows - HY, 0), HY)
+    u_ref[HX:HX + bx, pl.ds(start, HY)] = in_ref[0:bx]
+    for n, x, y, count in shared_planes(planes):
+        for c in range(bz // LANES):
+            cols = slice(LANES * c, LANES * c + LANES)
+            both = in_ref[bx + n, :, cols]
+            u_ref[x, pl.ds(start, HY), cols] = both
+            other = jnp.where(high, pltpu.roll(both, HY - count, 0), pltpu.roll(both, count, 0))
+            u_ref[y, pl.ds(start, HY), cols] = other
+
+
+def place_kernel(own_ref, u_ref):
     bx, by, bz = own_ref.shape
     planes = u_ref.shape[0]
+    u_ref[HX:HX + bx, HY:HY + by] = own_ref[...]
+    edge = jnp.zeros((1, HY, bz), F32)
+    for x in (0, planes - 1):
+        for y in (0, HY + by):
+            u_ref[x:x + 1, y:y + HY] = edge
+
+
+def join_kernel(mid_ref, first_ref, second_ref, u_ref, first_out, second_out):
+    bx, by, bz = first_ref.shape
     mine = slice(HY, HY + by)
     odd = parity("px")
     u_ref[pl.ds((1 - odd) * (HX + bx), HX), mine] = first_ref[pl.ds(odd * (bx - HX), HX)]
     u_ref[pl.ds(odd * (HX + bx), HX), mine] = second_ref[pl.ds((1 - odd) * (bx - HX), HX)]
-    u_ref[HX:HX + bx, mine] = own_ref[...]
     odd = parity("py")
-    u_ref[HX:HX + bx, pl.ds(pl.multiple_of(odd * (HY + by), HY), HY)] = rows_ref[...]
-    count = up_ref.shape[0]
-    high = pl.multiple_of(HY + (1 - odd) * (by - HY), HY)
-    low = pl.multiple_of(HY + odd * (by - HY), HY)
-    up_ref[...] = u_ref[1:1 + count, pl.ds(high, HY)]
-    row, _ = iotas()
-    full, pairs = strip_planes(planes)
-    for n, x in enumerate(full):
-        strip_ref[n] = u_ref[x, pl.ds(low, HY)]
-    for n, (x, y) in enumerate(pairs):
-        for c in range(bz // LANES):
-            cols = slice(LANES * c, LANES * c + LANES)
-            a = half_turn(u_ref[x, pl.ds(low, HY), cols], odd == 1)
-            b = half_turn(u_ref[y, pl.ds(low, HY), cols], odd == 0)
-            strip_ref[len(full) + n, :, cols] = jnp.where(row < 4, a, b)
-
-
-def first_kernel(mid_ref, up_ref, strip_ref, gap_ref, dist_ref, u_ref, w0, w1, w2, sums_ref):
-    planes, rows, bz = u_ref.shape
-    by = rows - 2 * HY
-    count = up_ref.shape[0]
+    pack_rows(u_ref, first_out, odd == 0)
+    pack_rows(u_ref, second_out, odd == 1)
+
+
+def first_kernel(mid_ref, first_ref, second_ref, gap_ref, dist_ref, u_ref, w0, w1, w2, sums_ref, q_ref):
+    planes = u_ref.shape[0]
     odd = parity("py")
-    edge = jnp.zeros((1, HY, bz), F32)
-    for x in (0, planes - 1):
-        for y in (0, HY + by):
-            u_ref[x:x + 1, y:y + HY] = edge
-    high = pl.multiple_of((1 - odd) * (HY + by), HY)
-    low = pl.multiple_of(odd * (HY + by), HY)
-    u_ref[1:1 + count, pl.ds(high, HY)] = up_ref[...]
-    full, pairs = strip_planes(planes)
-    for n, x in enumerate(full):
-        u_ref[x, pl.ds(low, HY)] = strip_ref[n]
-    for n, (x, y) in enumerate(pairs):
-        for c in range(bz // LANES):
-            cols = slice(LANES * c, LANES * c + LANES)
-            both = strip_ref[len(full) + n, :, cols]
-            u_ref[x, pl.ds(low, HY), cols] = half_turn(both, odd == 0)
-            u_ref[y, pl.ds(low, HY), cols] = half_turn(both, odd == 1)
-    krylov(u_ref, (w0, w1, w2), 1, planes - 1, None, (gap_ref, dist_ref), sums_ref)
-
-
-def second_kernel(cells, recv_ref, u_ref, a0, a1, a2, known_ref, v_ref, w0, w1, w2, sums_ref):
+    unpack_rows(first_ref, u_ref, odd == 0)
+    unpack_rows(second_ref, u_ref, odd == 1)
+    krylov(u_ref, (w0, w1, w2), q_ref, 1, planes - 1, None, (gap_ref, dist_ref), sums_ref)
+
+
+def second_kernel(cells, recv_ref, u_ref, a0, a1, a2, known_ref, v_ref, w0, w1, w2, sums_ref, q_ref):
     coef = coefficients(recv_ref, cells)
     planes = u_ref.shape[0]
     update(u_ref, (a0, a1, a2), coef, v_ref, 3, planes - 3)
-    krylov(v_ref, (w0, w1, w2), 4, planes - 4, known_ref, None, sums_ref)
-
-
-def third_kernel(cells, recv_ref, u_ref, a0, a1, a2, out_ref, res_ref, v_ref):
+    krylov(v_ref, (w0, w1, w2), q_ref, 4, planes - 4, known_ref, None, sums_ref)
+
+
+def third_kernel(cells, recv_ref, u_ref, a0, a1, a2, out_hbm, res_hbm, v_ref, out_ref, res_ref, sems):
     coef = coefficients(recv_ref, cells)
     planes, top = u_ref.shape[0], u_ref.shape[1] // 8
-    update(u_ref, (a0, a1, a2), coef, v_ref, HX - 1, planes - HX + 1)
+    update(u_ref, (a0, a1, a2), coef, v_ref, HX - 1, planes - HX + 1, out_ref)
+    field_copy = pltpu.make_async_copy(out_ref, out_hbm, sems.at[0])
+    field_copy.start()
     for x in range(HX, planes - HX):
         for t, c, v, total in plane_sums(v_ref, x, range(HY // 8, top - HY // 8)):
-            where = (x - HX, *tile(t - HY // 8, c))
-            out_ref[where] = v
-            res_ref[where] = 0.5 * total - v * (2.0 + v * v)
+            res_ref[(x - HX, *tile(t - HY // 8, c))] = 0.5 * total - v * (2.0 + v * v)
+    residual_copy = pltpu.make_async_copy(res_ref, res_hbm, sems.at[1])
+    residual_copy.start()
+    field_copy.wait()
+    residual_copy.wait()
 
 
 def total_over_devices(rows):
@@ -344,12 +354,12 @@
     params = pltpu.CompilerParams(vmem_limit_bytes=24 * 2**20)
     shape = lambda *dims: jax.ShapeDtypeStruct(dims, F32)
 
-    def call(body, name, outs, *args, scratch=(), alias={}):
+    def call(body, name, outs, *args, scratch=(), alias={}, space=pltpu.VMEM):
         return pl.pallas_call(
             body,
             out_shape=outs,
             in_specs=[vmem] * len(args),
-            out_specs=tuple(vmem for _ in outs),
+            out_specs=tuple(pl.BlockSpec(memory_space=space) for _ in outs),
             scratch_shapes=scratch,
             input_output_aliases=alias,
             compiler_params=params,
@@ -359,24 +369,25 @@
     planes, rows = bx + 2 * HX, by + 2 * HY
     own, whole = shape(bx, by, bz), shape(planes, rows, bz)
     sums = shape(devices, LANES)
+    room = pltpu.VMEM(whole.shape, F32)
     first, second = swap(start_field, "px", 0), swap(start_field, "px", 1)
-    (edge,) = call(edge_kernel, "edge", (shape(bx, HY, bz),), start_field)
-    edge = swap(edge, "py", 1)
-    full, pairs = strip_planes(planes)
-    parts = (whole, shape(planes - 2, HY, bz), shape(len(full) + len(pairs), HY, bz))
-    u, up, strip = call(join_kernel, "join", parts, start_field, first, second, edge)
-    up, strip = swap(up, "py", 0), swap(strip, "py", 1)
+    strip = shape(bx + 2 * len(SHARED), HY, bz)
+    (u,) = call(place_kernel, "place", (whole,), start_field)
+    u, first, second = call(join_kernel, "join", (whole, strip, strip), u, first, second, alias={0: 0})
+    first, second = swap(first, "py", 0), swap(second, "py", 1)
     parts = (shape(*known.shape), shape(*known.shape), shape(KNOWN, 8, LANES))
     known, gap, dist = call(gap_kernel, "gap", parts, start_field, known)
     step = (whole,) * 4 + (sums,)
-    u, a0, a1, a2, sent = call(first_kernel, "first_step", step, u, up, strip, gap, dist, alias={0: 0})
+    u, a0, a1, a2, sent = call(
+        first_kernel, "first_step", step, u, first, second, gap, dist, scratch=[room], alias={0: 0}
+    )
     recv = total_over_devices(sent)
     body = lambda *refs: second_kernel(cells, *refs)
-    v, b0, b1, b2, sent = call(body, "second_step", step, recv, u, a0, a1, a2, known)
+    v, b0, b1, b2, sent = call(body, "second_step", step, recv, u, a0, a1, a2, known, scratch=[room])
     recv = total_over_devices(sent)
     body = lambda *refs: third_kernel(cells, *refs)
-    scratch = [pltpu.VMEM(whole.shape, F32)]
-    field, residual = call(body, "finish", (own, own), recv, v, b0, b1, b2, scratch=scratch)
+    scratch = [room, pltpu.VMEM(own.shape, F32), pltpu.VMEM(own.shape, F32), pltpu.SemaphoreType.DMA((2,))]
+    field, residual = call(body, "finish", (own, own), recv, v, b0, b1, b2, scratch=scratch, space=pl.ANY)
     return field, residual
 
 

time: 75.8 us -> 76.1 us (level)
  starting transfers between devices: 13.9 us -> 9.04 us
  blocking collectives: 47.2 us -> 50.9 us
  waiting for transfers between devices: 3.25 us -> 6.84 us
  local copies, waits for them, and re-layouts: 2.57 us -> 0.95 us
    ppermute x5 -> x4, starting transfers between devices: 13.9 us -> 9.04 us  [swap(): return lax.ppermute(part, axis, pairs)]
    all_to_all x2, blocking collectives: 47.2 us -> 50.9 us  [total_over_devices(): return lax.all_to_all(rows, AXES, 0, 0).reshape(count, LANES)]
    ppermute x5 -> x4, waiting for transfers between devices: 3.25 us -> 6.84 us  [swap(): return lax.ppermute(part, axis, pairs)]
    unnamed x4, local copies, waits for them, and re-layouts: 2.57 us -> 0.95 us
  transfers between devices with their start and end apart: 5 -> 4, of which waited for: 2 -> 2; matrix products, arithmetic and copies ran while one was open for 0% -> 0% of each run, Pallas kernels for 1% -> 1%
where the time goes in v5:
time: 76.1 us; the launch traced here: 75.9 us
  blocking collectives  50.9 us (67%)
  starting transfers between devices  9.04 us (12%)
  Pallas kernels  7.48 us (10%)
  waiting for transfers between devices  6.84 us (9%)
  local copies, waits for them, and re-layouts  0.95 us (1%)
    all_to_all x2, blocking collectives, total_over_devices(): return lax.all_to_all(rows, AXES, 0, 0).reshape(count, LANES)  50.9 us
    ppermute x4, starting transfers between devices, swap(): return lax.ppermute(part, axis, pairs)  9.04 us
    pallas_call x6, Pallas kernels, call(): pl.pallas_call(body, out_shape=outs, in_specs=[vmem] * len(args), out_spe...  7.48 us
    ppermute x4, waiting for transfers between devices, swap(): return lax.ppermute(part, axis, pairs)  6.84 us
  transfers between devices with their start and end apart: 4, of which 2 were waited for; matrix products, arithmetic and copies ran while one was open for 0% of the time, Pallas kernels for 1%

profile of v5, /device:TPU:1, one launch (start us, length us, event | category | flops | bytes accessed | tf_op | source)
XLA Modules:
  0.0 75.9 jit_solution(6074489158585314430)
XLA Ops:
  0.6 0.0 copy-start
  0.6 2.1 %collective-permute-start = (f32[8,16,512]{2,1,0:T(8,128)}, f32[8,16,512]{2,1,0:T(8,128)S(1)}, u32[]{:S(2)}, u32[]{:S(2)}) collective-permute-start(f32[8,16,512]{2,1,0:T(8,128)} %field_ref.1), channel_id=1, source_target_pairs={{0,16},{16,0},{32,48},{48,32},{64,80},{80,64},{96,112},{112,96},{1... | collective-permute-start | bytes 786440 | tf_op jit(solution)/shard_map/ppermute | solution.py:346
  2.8 0.7 collective-permute-start.1
  3.4 0.0 copy-start.1
  3.5 0.9 %copy-done.1 = f32[8,16,512]{2,1,0:T(8,128)S(1)} copy-done((f32[8,16,512]{2,1,0:T(8,128)S(1)}, f32[8,16,512]{2,1,0:T(8,128)}, u32[]{:S(2)}) %copy-start.1) | copy-done | bytes 262168
  4.4 3.4 %collective-permute-done.first_ref = f32[8,16,512]{2,1,0:T(8,128)S(1)} collective-permute-done((f32[8,16,512]{2,1,0:T(8,128)}, f32[8,16,512]{2,1,0:T(8,128)S(1)}, u32[]{:S(2)}, u32[]{:S(2)}) %collective-permute-start) | collective-permute-done | bytes 262176 | tf_op jit(solution)/shard_map/ppermute | solution.py:346
  7.8 0.0 collective-permute-done.1.second_ref
  7.8 0.1 join.1
  7.9 2.9 %collective-permute-start.2 = (f32[14,8,512]{2,1,0:T(8,128)S(1)}, f32[14,8,512]{2,1,0:T(8,128)S(1)}, u32[]{:S(2)}, u32[]{:S(2)}) collective-permute-start(f32[14,8,512]{2,1,0:T(8,128)S(1)} %get-tuple-element.19), channel_id=1, source_target_pairs={{0,1},{1,0},{2,3},{3,2},{4,5},{5,4},{6,7},{7,6},{8,9},{9,8},{10,11... | collective-permute-start | bytes 688136 | tf_op jit(solution)/shard_map/ppermute | solution.py:346
  10.7 3.4 %collective-permute-start.3 = (f32[14,8,512]{2,1,0:T(8,128)S(1)}, f32[14,8,512]{2,1,0:T(8,128)S(1)}, u32[]{:S(2)}, u32[]{:S(2)}) collective-permute-start(f32[14,8,512]{2,1,0:T(8,128)S(1)} %get-tuple-element.20), channel_id=1, source_target_pairs={{1,2},{2,1},{3,4},{4,3},{5,6},{6,5},{7,8},{8,7},{9,10},{10,9},{11,... | collective-permute-start | bytes 688136 | tf_op jit(solution)/shard_map/ppermute | solution.py:346
  14.1 0.0 copy-done
  14.1 0.4 gap.1
  14.6 0.0 collective-permute-done.2.first_ref
  14.6 3.5 %collective-permute-done.3.second_ref = f32[14,8,512]{2,1,0:T(8,128)S(1)} collective-permute-done((f32[14,8,512]{2,1,0:T(8,128)S(1)}, f32[14,8,512]{2,1,0:T(8,128)S(1)}, u32[]{:S(2)}, u32[]{:S(2)}) %collective-permute-start.3) | collective-permute-done | bytes 229408 | tf_op jit(solution)/shard_map/ppermute | solution.py:346
  18.0 2.8 %first_step.1 = (f32[22,32,512]{2,1,0:T(8,128)S(1)}, f32[22,32,512]{2,1,0:T(8,128)S(1)}, f32[22,32,512]{2,1,0:T(8,128)S(1)}, f32[22,32,512]{2,1,0:T(8,128)S(1)}, f32[256,128]{1,0:T(8,128)S(1)}) custom-call(f32[22,32,512]{2,1,0:T(8,128)S(1)} %get-tuple-element.18.mid_ref, ...), custom_call_target="tpu_custom_call", output_to_operand_aliasing={{0}: (0, {})} | custom-call | tf_op jit(solution)/shard_map/first_step/pallas_call | solution.py:358
  20.9 32.3 %all_to_all.10 = f32[256,1,128]{2,1,0:T(1,128)S(1)} all-to-all(f32[256,1,128]{2,1,0:T(1,128)S(1)} %bitcast.11), channel_id=1, replica_groups=mesh['px'=16,'py'=16] {'px','py'}, dimensions={0} | all-to-all | bytes 262144 | tf_op jit(solution)/shard_map/all_to_all | solution.py:339
  53.2 2.8 %second_step.1 = (f32[22,32,512]{2,1,0:T(8,128)S(1)}, f32[22,32,512]{2,1,0:T(8,128)S(1)}, f32[22,32,512]{2,1,0:T(8,128)S(1)}, f32[22,32,512]{2,1,0:T(8,128)S(1)}, f32[256,128]{1,0:T(8,128)S(1)}) custom-call(f32[256,128]{1,0:T(8,128)S(1)} %bitcast.8, f32[22,32,512]{2,1,0:T(8,128)S(1)} %get-tuple-element.24.refs_1_, ...), custom_call_target="tpu_custom_call" | custom-call | tf_op jit(solution)/shard_map/second_step/pallas_call | solution.py:358
  56.0 18.6 %all_to_all.11 = f32[256,1,128]{2,1,0:T(1,128)S(1)} all-to-all(f32[256,1,128]{2,1,0:T(1,128)S(1)} %bitcast.10), channel_id=1, replica_groups=mesh['px'=16,'py'=16] {'px','py'}, dimensions={0} | all-to-all | bytes 262144 | tf_op jit(solution)/shard_map/all_to_all | solution.py:339
  74.6 1.3 %finish.1 = (f32[8,16,512]{2,1,0:T(8,128)}, f32[8,16,512]{2,1,0:T(8,128)}) custom-call(f32[256,128]{1,0:T(8,128)S(1)} %bitcast.9, f32[22,32,512]{2,1,0:T(8,128)S(1)} %get-tuple-element.30.refs_1_, f32[22,32,512]{2,1,0:T(8,128)S(1)} %get-tuple-element.31.refs_2_, f32[22,32,512]{2,1,0:T(8,128)S(1)} %get-tuple-element.32.refs_3_, ...), custom_call_target="tpu_custom_call" | custom-call | tf_op jit(solution)/shard_map/finish/pallas_call | solution.py:358
  (1 shorter events, 0.0 us)
Async XLA Ops:
  0.6 13.5 %copy-start = (f32[8,8,16,512]{3,2,1,0:T(8,128)S(1)}, f32[8,8,16,512]{3,2,1,0:T(8,128)}, u32[]{:S(2)}) copy-start(f32[8,8,16,512]{3,2,1,0:T(8,128)} %known_ref.1) | copy-start | bytes 6291460
  0.6 7.1 %collective-permute-start = (f32[8,16,512]{2,1,0:T(8,128)}, f32[8,16,512]{2,1,0:T(8,128)S(1)}, u32[]{:S(2)}, u32[]{:S(2)}) collective-permute-start(f32[8,16,512]{2,1,0:T(8,128)} %field_ref.1), channel_id=1, source_target_pairs={{0,16},{16,0},{32,48},{48,32},{64,80},{80,64},{96,112},{112,96},{1... | collective-permute-start | bytes 786440 | tf_op jit(solution)/shard_map/ppermute | solution.py:346
  2.8 5.0 %collective-permute-start.1 = (f32[8,16,512]{2,1,0:T(8,128)}, f32[8,16,512]{2,1,0:T(8,128)S(1)}, u32[]{:S(2)}, u32[]{:S(2)}) collective-permute-start(f32[8,16,512]{2,1,0:T(8,128)} %field_ref.1), channel_id=1, source_target_pairs={{16,32},{32,16},{48,64},{64,48},{80,96},{96,80},{112,128},{128,112... | collective-permute-start | bytes 786440 | tf_op jit(solution)/shard_map/ppermute | solution.py:346
  3.4 1.0 %copy-start.1 = (f32[8,16,512]{2,1,0:T(8,128)S(1)}, f32[8,16,512]{2,1,0:T(8,128)}, u32[]{:S(2)}) copy-start(f32[8,16,512]{2,1,0:T(8,128)} %field_ref.1) | copy-start | bytes 786436
  7.9 6.7 %collective-permute-start.2 = (f32[14,8,512]{2,1,0:T(8,128)S(1)}, f32[14,8,512]{2,1,0:T(8,128)S(1)}, u32[]{:S(2)}, u32[]{:S(2)}) collective-permute-start(f32[14,8,512]{2,1,0:T(8,128)S(1)} %get-tuple-element.19), channel_id=1, source_target_pairs={{0,1},{1,0},{2,3},{3,2},{4,5},{5,4},{6,7},{7,6},{8,9},{9,8},{10,11... | collective-permute-start | bytes 688136 | tf_op jit(solution)/shard_map/ppermute | solution.py:346
  10.7 7.3 %collective-permute-start.3 = (f32[14,8,512]{2,1,0:T(8,128)S(1)}, f32[14,8,512]{2,1,0:T(8,128)S(1)}, u32[]{:S(2)}, u32[]{:S(2)}) collective-permute-start(f32[14,8,512]{2,1,0:T(8,128)S(1)} %get-tuple-element.20), channel_id=1, source_target_pairs={{1,2},{2,1},{3,4},{4,3},{5,6},{6,5},{7,8},{8,7},{9,10},{10,9},{11,... | collective-permute-start | bytes 688136 | tf_op jit(solution)/shard_map/ppermute | solution.py:346

commit v6 on v5

--- a/solution.py
+++ b/solution.py
@@ -292,7 +292,7 @@
             u_ref[x:x + 1, y:y + HY] = edge
 
 
-def join_kernel(mid_ref, first_ref, second_ref, u_ref, first_out, second_out):
+def join_kernel(mid_ref, second_ref, first_ref, u_ref, first_out, second_out):
     bx, by, bz = first_ref.shape
     mine = slice(HY, HY + by)
     odd = parity("px")
@@ -303,7 +303,7 @@
     pack_rows(u_ref, second_out, odd == 1)
 
 
-def first_kernel(mid_ref, first_ref, second_ref, gap_ref, dist_ref, u_ref, w0, w1, w2, sums_ref, q_ref):
+def first_kernel(mid_ref, second_ref, first_ref, gap_ref, dist_ref, u_ref, w0, w1, w2, sums_ref, q_ref):
     planes = u_ref.shape[0]
     odd = parity("py")
     unpack_rows(first_ref, u_ref, odd == 0)
@@ -370,16 +370,18 @@
     own, whole = shape(bx, by, bz), shape(planes, rows, bz)
     sums = shape(devices, LANES)
     room = pltpu.VMEM(whole.shape, F32)
-    first, second = swap(start_field, "px", 0), swap(start_field, "px", 1)
+    second = swap(start_field, "px", 1)
+    first = swap(start_field, "px", 0)
     strip = shape(bx + 2 * len(SHARED), HY, bz)
     (u,) = call(place_kernel, "place", (whole,), start_field)
-    u, first, second = call(join_kernel, "join", (whole, strip, strip), u, first, second, alias={0: 0})
-    first, second = swap(first, "py", 0), swap(second, "py", 1)
+    u, first, second = call(join_kernel, "join", (whole, strip, strip), u, second, first, alias={0: 0})
+    second = swap(second, "py", 1)
+    first = swap(first, "py", 0)
     parts = (shape(*known.shape), shape(*known.shape), shape(KNOWN, 8, LANES))
     known, gap, dist = call(gap_kernel, "gap", parts, start_field, known)
     step = (whole,) * 4 + (sums,)
     u, a0, a1, a2, sent = call(
-        first_kernel, "first_step", step, u, first, second, gap, dist, scratch=[room], alias={0: 0}
+        first_kernel, "first_step", step, u, second, first, gap, dist, scratch=[room], alias={0: 0}
     )
     recv = total_over_devices(sent)
     body = lambda *refs: second_kernel(cells, *refs)

time: 76.1 us -> 75.6 us (level)
  blocking collectives: 50.9 us -> 47.7 us
  starting transfers between devices: 9.04 us -> 10.4 us
  waiting for transfers between devices: 6.84 us -> 8.04 us
    all_to_all x2, blocking collectives: 50.9 us -> 47.7 us  [total_over_devices(): return lax.all_to_all(rows, AXES, 0, 0).reshape(count, LANES)]
    ppermute x4, starting transfers between devices: 9.04 us -> 10.4 us  [swap(): return lax.ppermute(part, axis, pairs)]
    ppermute x4, waiting for transfers between devices: 6.84 us -> 8.04 us  [swap(): return lax.ppermute(part, axis, pairs)]
where the time goes in v6:
time: 75.6 us; the launch traced here: 75.3 us
  blocking collectives  47.7 us (63%)
  starting transfers between devices  10.4 us (14%)
  waiting for transfers between devices  8.04 us (11%)
  Pallas kernels  7.48 us (10%)
  local copies, waits for them, and re-layouts  0.99 us (1%)
    all_to_all x2, blocking collectives, total_over_devices(): return lax.all_to_all(rows, AXES, 0, 0).reshape(count, LANES)  47.7 us
    ppermute x4, starting transfers between devices, swap(): return lax.ppermute(part, axis, pairs)  10.4 us
    ppermute x4, waiting for transfers between devices, swap(): return lax.ppermute(part, axis, pairs)  8.04 us
    pallas_call x6, Pallas kernels, call(): pl.pallas_call(body, out_shape=outs, in_specs=[vmem] * len(args), out_spe...  7.48 us
  transfers between devices with their start and end apart: 4, of which 2 were waited for; matrix products, arithmetic and copies ran while one was open for 0% of the time, Pallas kernels for 1%

profile of v6, /device:TPU:1, one launch (start us, length us, event | category | flops | bytes accessed | tf_op | source)
XLA Modules:
  0.0 75.3 jit_solution(5306531166749741379)
XLA Ops:
  0.6 0.0 copy-start
  0.6 0.8 %collective-permute-start = (f32[8,16,512]{2,1,0:T(8,128)}, f32[8,16,512]{2,1,0:T(8,128)S(1)}, u32[]{:S(2)}, u32[]{:S(2)}) collective-permute-start(f32[8,16,512]{2,1,0:T(8,128)} %field_ref.1), channel_id=1, source_target_pairs={{16,32},{32,16},{48,64},{64,48},{80,96},{96,80},{112,128},{128,112... | collective-permute-start | bytes 786440 | tf_op jit(solution)/shard_map/ppermute | solution.py:346
  1.5 4.6 %collective-permute-start.1 = (f32[8,16,512]{2,1,0:T(8,128)}, f32[8,16,512]{2,1,0:T(8,128)S(1)}, u32[]{:S(2)}, u32[]{:S(2)}) collective-permute-start(f32[8,16,512]{2,1,0:T(8,128)} %field_ref.1), channel_id=1, source_target_pairs={{0,16},{16,0},{32,48},{48,32},{64,80},{80,64},{96,112},{112,96},{1... | collective-permute-start | bytes 786440 | tf_op jit(solution)/shard_map/ppermute | solution.py:346
  6.0 0.0 copy-start.1
  6.0 1.0 %copy-done.1 = f32[8,16,512]{2,1,0:T(8,128)S(1)} copy-done((f32[8,16,512]{2,1,0:T(8,128)S(1)}, f32[8,16,512]{2,1,0:T(8,128)}, u32[]{:S(2)}) %copy-start.1) | copy-done | bytes 262168
  7.0 0.0 collective-permute-done.second_ref
  7.0 4.9 %collective-permute-done.1.first_ref = f32[8,16,512]{2,1,0:T(8,128)S(1)} collective-permute-done((f32[8,16,512]{2,1,0:T(8,128)}, f32[8,16,512]{2,1,0:T(8,128)S(1)}, u32[]{:S(2)}, u32[]{:S(2)}) %collective-permute-start.1) | collective-permute-done | bytes 262176 | tf_op jit(solution)/shard_map/ppermute | solution.py:346
  11.9 0.1 join.1
  12.0 5.0 %collective-permute-start.2 = (f32[14,8,512]{2,1,0:T(8,128)S(1)}, f32[14,8,512]{2,1,0:T(8,128)S(1)}, u32[]{:S(2)}, u32[]{:S(2)}) collective-permute-start(f32[14,8,512]{2,1,0:T(8,128)S(1)} %get-tuple-element.19), channel_id=1, source_target_pairs={{1,2},{2,1},{3,4},{4,3},{5,6},{6,5},{7,8},{8,7},{9,10},{10,9},{11,... | collective-permute-start | bytes 688136 | tf_op jit(solution)/shard_map/ppermute | solution.py:346
  17.0 0.1 collective-permute-start.3
  17.1 0.0 copy-done
  17.1 0.4 gap.1
  17.6 3.1 %collective-permute-done.2.second_ref = f32[14,8,512]{2,1,0:T(8,128)S(1)} collective-permute-done((f32[14,8,512]{2,1,0:T(8,128)S(1)}, f32[14,8,512]{2,1,0:T(8,128)S(1)}, u32[]{:S(2)}, u32[]{:S(2)}) %collective-permute-start.2) | collective-permute-done | bytes 229408 | tf_op jit(solution)/shard_map/ppermute | solution.py:346
  20.7 0.0 collective-permute-done.3.first_ref
  20.7 2.8 %first_step.1 = (f32[22,32,512]{2,1,0:T(8,128)S(1)}, f32[22,32,512]{2,1,0:T(8,128)S(1)}, f32[22,32,512]{2,1,0:T(8,128)S(1)}, f32[22,32,512]{2,1,0:T(8,128)S(1)}, f32[256,128]{1,0:T(8,128)S(1)}) custom-call(f32[22,32,512]{2,1,0:T(8,128)S(1)} %get-tuple-element.18.mid_ref, ...), custom_call_target="tpu_custom_call", output_to_operand_aliasing={{0}: (0, {})} | custom-call | tf_op jit(solution)/shard_map/first_step/pallas_call | solution.py:358
  23.5 29.1 %all_to_all.10 = f32[256,1,128]{2,1,0:T(1,128)S(1)} all-to-all(f32[256,1,128]{2,1,0:T(1,128)S(1)} %bitcast.11), channel_id=1, replica_groups=mesh['px'=16,'py'=16] {'px','py'}, dimensions={0} | all-to-all | bytes 262144 | tf_op jit(solution)/shard_map/all_to_all | solution.py:339
  52.6 2.8 %second_step.1 = (f32[22,32,512]{2,1,0:T(8,128)S(1)}, f32[22,32,512]{2,1,0:T(8,128)S(1)}, f32[22,32,512]{2,1,0:T(8,128)S(1)}, f32[22,32,512]{2,1,0:T(8,128)S(1)}, f32[256,128]{1,0:T(8,128)S(1)}) custom-call(f32[256,128]{1,0:T(8,128)S(1)} %bitcast.8, f32[22,32,512]{2,1,0:T(8,128)S(1)} %get-tuple-element.24.refs_1_, ...), custom_call_target="tpu_custom_call" | custom-call | tf_op jit(solution)/shard_map/second_step/pallas_call | solution.py:358
  55.4 18.6 %all_to_all.11 = f32[256,1,128]{2,1,0:T(1,128)S(1)} all-to-all(f32[256,1,128]{2,1,0:T(1,128)S(1)} %bitcast.10), channel_id=1, replica_groups=mesh['px'=16,'py'=16] {'px','py'}, dimensions={0} | all-to-all | bytes 262144 | tf_op jit(solution)/shard_map/all_to_all | solution.py:339
  74.0 1.3 %finish.1 = (f32[8,16,512]{2,1,0:T(8,128)}, f32[8,16,512]{2,1,0:T(8,128)}) custom-call(f32[256,128]{1,0:T(8,128)S(1)} %bitcast.9, f32[22,32,512]{2,1,0:T(8,128)S(1)} %get-tuple-element.30.refs_1_, f32[22,32,512]{2,1,0:T(8,128)S(1)} %get-tuple-element.31.refs_2_, f32[22,32,512]{2,1,0:T(8,128)S(1)} %get-tuple-element.32.refs_3_, ...), custom_call_target="tpu_custom_call" | custom-call | tf_op jit(solution)/shard_map/finish/pallas_call | solution.py:358
  (1 shorter events, 0.0 us)
Async XLA Ops:
  0.6 16.5 %copy-start = (f32[8,8,16,512]{3,2,1,0:T(8,128)S(1)}, f32[8,8,16,512]{3,2,1,0:T(8,128)}, u32[]{:S(2)}) copy-start(f32[8,8,16,512]{3,2,1,0:T(8,128)} %known_ref.1) | copy-start | bytes 6291460
  0.6 6.4 %collective-permute-start = (f32[8,16,512]{2,1,0:T(8,128)}, f32[8,16,512]{2,1,0:T(8,128)S(1)}, u32[]{:S(2)}, u32[]{:S(2)}) collective-permute-start(f32[8,16,512]{2,1,0:T(8,128)} %field_ref.1), channel_id=1, source_target_pairs={{16,32},{32,16},{48,64},{64,48},{80,96},{96,80},{112,128},{128,112... | collective-permute-start | bytes 786440 | tf_op jit(solution)/shard_map/ppermute | solution.py:346
  1.5 10.5 %collective-permute-start.1 = (f32[8,16,512]{2,1,0:T(8,128)}, f32[8,16,512]{2,1,0:T(8,128)S(1)}, u32[]{:S(2)}, u32[]{:S(2)}) collective-permute-start(f32[8,16,512]{2,1,0:T(8,128)} %field_ref.1), channel_id=1, source_target_pairs={{0,16},{16,0},{32,48},{48,32},{64,80},{80,64},{96,112},{112,96},{1... | collective-permute-start | bytes 786440 | tf_op jit(solution)/shard_map/ppermute | solution.py:346
  6.0 1.0 %copy-start.1 = (f32[8,16,512]{2,1,0:T(8,128)S(1)}, f32[8,16,512]{2,1,0:T(8,128)}, u32[]{:S(2)}) copy-start(f32[8,16,512]{2,1,0:T(8,128)} %field_ref.1) | copy-start | bytes 786436
  12.0 8.7 %collective-permute-start.2 = (f32[14,8,512]{2,1,0:T(8,128)S(1)}, f32[14,8,512]{2,1,0:T(8,128)S(1)}, u32[]{:S(2)}, u32[]{:S(2)}) collective-permute-start(f32[14,8,512]{2,1,0:T(8,128)S(1)} %get-tuple-element.19), channel_id=1, source_target_pairs={{1,2},{2,1},{3,4},{4,3},{5,6},{6,5},{7,8},{8,7},{9,10},{10,9},{11,... | collective-permute-start | bytes 688136 | tf_op jit(solution)/shard_map/ppermute | solution.py:346
  17.0 3.7 %collective-permute-start.3 = (f32[14,8,512]{2,1,0:T(8,128)S(1)}, f32[14,8,512]{2,1,0:T(8,128)S(1)}, u32[]{:S(2)}, u32[]{:S(2)}) collective-permute-start(f32[14,8,512]{2,1,0:T(8,128)S(1)} %get-tuple-element.20), channel_id=1, source_target_pairs={{0,1},{1,0},{2,3},{3,2},{4,5},{5,4},{6,7},{7,6},{8,9},{9,8},{10,11... | collective-permute-start | bytes 688136 | tf_op jit(solution)/shard_map/ppermute | solution.py:346

commit v7 on v6

--- a/solution.py
+++ b/solution.py
@@ -6,6 +6,7 @@
 from jax.sharding import PartitionSpec as P
 
 EPS = 1e-06
+NOISE = 1e-07
 DEFLATE = 4.0
 ITERS = 3
 KNOWN = 8
@@ -77,7 +78,7 @@
                 where = (x, *tile(t, c))
                 if k == 0:
                     square = v * v
-                    q_ref[where] = 2.0 - 6.0 * square
+                    q_ref[where] = -1.0 - 6.0 * square
                     value = total - v * (4.0 + 2.0 * square)
                 else:
                     value = total + q_ref[where] * v
@@ -122,7 +123,9 @@
     mu = [jnp.broadcast_to(line[:, n:n + 1], (8, LANES)) for n in range(7)]
     zero = jnp.zeros((8, LANES), F32)
 
-    def inner(p, q):
+    size = [jnp.abs(m) for m in mu]
+
+    def inner(p, q, mu=mu):
         total = None
         for i, a in enumerate(p):
             if a is None:
@@ -145,7 +148,7 @@
         image = [None] * (k + 2)
         for i in range(k + 2):
             a = 0.5 * vec[i - 1] if i > 0 else None
-            b = -3.0 * vec[i] if i <= k else None
+            b = -1.5 * vec[i] if i <= k else None
             image[i] = b if a is None else (a if b is None else a + b)
         for j in range(k + 1):
             hess[j, k] = inner(basis[j], image)
@@ -153,10 +156,13 @@
         for j in range(k + 1):
             for i in range(len(basis[j])):
                 rest[i] = rest[i] - hess[j, k] * basis[j][i]
-        square = jnp.maximum(inner(rest, rest), 0.0)
+        square = inner(rest, rest)
+        lengths = [jnp.abs(a) for a in rest]
+        sound = square > NOISE * inner(lengths, lengths, size)
+        square = jnp.where(sound, square, 0.0)
         hess[k + 1, k] = jnp.sqrt(square + EPS)
         if k < ITERS - 1:
-            scale = 1.0 / hess[k + 1, k]
+            scale = jnp.where(sound, 1.0 / hess[k + 1, k], 0.0)
             basis.append([a * scale for a in rest])
 
     def normal(i, j):
@@ -172,6 +178,7 @@
         diag = normal(j, j)
         for r in range(j):
             diag = diag - lower[j, r] * lower[j, r]
+        diag = jnp.maximum(diag, hess[j + 1, j] * hess[j + 1, j])
         lower[j, j] = jnp.sqrt(diag)
         for i in range(j + 1, ITERS):
             off = normal(i, j)

time: 75.6 us -> 75.6 us (level)
  no operation moved by 1% of the time
where the time goes in v7:
time: 75.6 us; the launch traced here: 75.4 us
  blocking collectives  47.7 us (63%)
  starting transfers between devices  10.4 us (14%)
  waiting for transfers between devices  8.04 us (11%)
  Pallas kernels  7.51 us (10%)
  local copies, waits for them, and re-layouts  0.99 us (1%)
    all_to_all x2, blocking collectives, total_over_devices(): return lax.all_to_all(rows, AXES, 0, 0).reshape(count, LANES)  47.7 us
    ppermute x4, starting transfers between devices, swap(): return lax.ppermute(part, axis, pairs)  10.4 us
    ppermute x4, waiting for transfers between devices, swap(): return lax.ppermute(part, axis, pairs)  8.04 us
    pallas_call x6, Pallas kernels, call(): pl.pallas_call(body, out_shape=outs, in_specs=[vmem] * len(args), out_spe...  7.51 us
  transfers between devices with their start and end apart: 4, of which 2 were waited for; matrix products, arithmetic and copies ran while one was open for 0% of the time, Pallas kernels for 1%

profile of v7, /device:TPU:1, one launch (start us, length us, event | category | flops | bytes accessed | tf_op | source)
XLA Modules:
  0.0 75.4 jit_solution(17306157066214561006)
XLA Ops:
  0.6 0.0 copy-start
  0.6 0.8 %collective-permute-start = (f32[8,16,512]{2,1,0:T(8,128)}, f32[8,16,512]{2,1,0:T(8,128)S(1)}, u32[]{:S(2)}, u32[]{:S(2)}) collective-permute-start(f32[8,16,512]{2,1,0:T(8,128)} %field_ref.1), channel_id=1, source_target_pairs={{16,32},{32,16},{48,64},{64,48},{80,96},{96,80},{112,128},{128,112... | collective-permute-start | bytes 786440 | tf_op jit(solution)/shard_map/ppermute | solution.py:353
  1.5 4.6 %collective-permute-start.1 = (f32[8,16,512]{2,1,0:T(8,128)}, f32[8,16,512]{2,1,0:T(8,128)S(1)}, u32[]{:S(2)}, u32[]{:S(2)}) collective-permute-start(f32[8,16,512]{2,1,0:T(8,128)} %field_ref.1), channel_id=1, source_target_pairs={{0,16},{16,0},{32,48},{48,32},{64,80},{80,64},{96,112},{112,96},{1... | collective-permute-start | bytes 786440 | tf_op jit(solution)/shard_map/ppermute | solution.py:353
  6.0 0.0 copy-start.1
  6.0 1.0 %copy-done.1 = f32[8,16,512]{2,1,0:T(8,128)S(1)} copy-done((f32[8,16,512]{2,1,0:T(8,128)S(1)}, f32[8,16,512]{2,1,0:T(8,128)}, u32[]{:S(2)}) %copy-start.1) | copy-done | bytes 262168
  7.0 0.0 collective-permute-done.second_ref
  7.0 4.9 %collective-permute-done.1.first_ref = f32[8,16,512]{2,1,0:T(8,128)S(1)} collective-permute-done((f32[8,16,512]{2,1,0:T(8,128)}, f32[8,16,512]{2,1,0:T(8,128)S(1)}, u32[]{:S(2)}, u32[]{:S(2)}) %collective-permute-start.1) | collective-permute-done | bytes 262176 | tf_op jit(solution)/shard_map/ppermute | solution.py:353
  11.9 0.1 join.1
  12.0 5.0 %collective-permute-start.2 = (f32[14,8,512]{2,1,0:T(8,128)S(1)}, f32[14,8,512]{2,1,0:T(8,128)S(1)}, u32[]{:S(2)}, u32[]{:S(2)}) collective-permute-start(f32[14,8,512]{2,1,0:T(8,128)S(1)} %get-tuple-element.19), channel_id=1, source_target_pairs={{1,2},{2,1},{3,4},{4,3},{5,6},{6,5},{7,8},{8,7},{9,10},{10,9},{11,... | collective-permute-start | bytes 688136 | tf_op jit(solution)/shard_map/ppermute | solution.py:353
  17.0 0.1 collective-permute-start.3
  17.1 0.0 copy-done
  17.1 0.4 gap.1
  17.6 3.1 %collective-permute-done.2.second_ref = f32[14,8,512]{2,1,0:T(8,128)S(1)} collective-permute-done((f32[14,8,512]{2,1,0:T(8,128)S(1)}, f32[14,8,512]{2,1,0:T(8,128)S(1)}, u32[]{:S(2)}, u32[]{:S(2)}) %collective-permute-start.2) | collective-permute-done | bytes 229408 | tf_op jit(solution)/shard_map/ppermute | solution.py:353
  20.7 0.0 collective-permute-done.3.first_ref
  20.7 2.8 %first_step.1 = (f32[22,32,512]{2,1,0:T(8,128)S(1)}, f32[22,32,512]{2,1,0:T(8,128)S(1)}, f32[22,32,512]{2,1,0:T(8,128)S(1)}, f32[22,32,512]{2,1,0:T(8,128)S(1)}, f32[256,128]{1,0:T(8,128)S(1)}) custom-call(f32[22,32,512]{2,1,0:T(8,128)S(1)} %get-tuple-element.18.mid_ref, ...), custom_call_target="tpu_custom_call", output_to_operand_aliasing={{0}: (0, {})} | custom-call | tf_op jit(solution)/shard_map/first_step/pallas_call | solution.py:365
  23.5 29.1 %all_to_all.10 = f32[256,1,128]{2,1,0:T(1,128)S(1)} all-to-all(f32[256,1,128]{2,1,0:T(1,128)S(1)} %bitcast.11), channel_id=1, replica_groups=mesh['px'=16,'py'=16] {'px','py'}, dimensions={0} | all-to-all | bytes 262144 | tf_op jit(solution)/shard_map/all_to_all | solution.py:346
  52.6 2.8 %second_step.1 = (f32[22,32,512]{2,1,0:T(8,128)S(1)}, f32[22,32,512]{2,1,0:T(8,128)S(1)}, f32[22,32,512]{2,1,0:T(8,128)S(1)}, f32[22,32,512]{2,1,0:T(8,128)S(1)}, f32[256,128]{1,0:T(8,128)S(1)}) custom-call(f32[256,128]{1,0:T(8,128)S(1)} %bitcast.8, f32[22,32,512]{2,1,0:T(8,128)S(1)} %get-tuple-element.24.refs_1_, ...), custom_call_target="tpu_custom_call" | custom-call | tf_op jit(solution)/shard_map/second_step/pallas_call | solution.py:365
  55.4 18.6 %all_to_all.11 = f32[256,1,128]{2,1,0:T(1,128)S(1)} all-to-all(f32[256,1,128]{2,1,0:T(1,128)S(1)} %bitcast.10), channel_id=1, replica_groups=mesh['px'=16,'py'=16] {'px','py'}, dimensions={0} | all-to-all | bytes 262144 | tf_op jit(solution)/shard_map/all_to_all | solution.py:346
  74.0 1.3 %finish.1 = (f32[8,16,512]{2,1,0:T(8,128)}, f32[8,16,512]{2,1,0:T(8,128)}) custom-call(f32[256,128]{1,0:T(8,128)S(1)} %bitcast.9, f32[22,32,512]{2,1,0:T(8,128)S(1)} %get-tuple-element.30.refs_1_, f32[22,32,512]{2,1,0:T(8,128)S(1)} %get-tuple-element.31.refs_2_, f32[22,32,512]{2,1,0:T(8,128)S(1)} %get-tuple-element.32.refs_3_, ...), custom_call_target="tpu_custom_call" | custom-call | tf_op jit(solution)/shard_map/finish/pallas_call | solution.py:365
  (1 shorter events, 0.0 us)
Async XLA Ops:
  0.6 16.5 %copy-start = (f32[8,8,16,512]{3,2,1,0:T(8,128)S(1)}, f32[8,8,16,512]{3,2,1,0:T(8,128)}, u32[]{:S(2)}) copy-start(f32[8,8,16,512]{3,2,1,0:T(8,128)} %known_ref.1) | copy-start | bytes 6291460
  0.6 6.4 %collective-permute-start = (f32[8,16,512]{2,1,0:T(8,128)}, f32[8,16,512]{2,1,0:T(8,128)S(1)}, u32[]{:S(2)}, u32[]{:S(2)}) collective-permute-start(f32[8,16,512]{2,1,0:T(8,128)} %field_ref.1), channel_id=1, source_target_pairs={{16,32},{32,16},{48,64},{64,48},{80,96},{96,80},{112,128},{128,112... | collective-permute-start | bytes 786440 | tf_op jit(solution)/shard_map/ppermute | solution.py:353
  1.5 10.5 %collective-permute-start.1 = (f32[8,16,512]{2,1,0:T(8,128)}, f32[8,16,512]{2,1,0:T(8,128)S(1)}, u32[]{:S(2)}, u32[]{:S(2)}) collective-permute-start(f32[8,16,512]{2,1,0:T(8,128)} %field_ref.1), channel_id=1, source_target_pairs={{0,16},{16,0},{32,48},{48,32},{64,80},{80,64},{96,112},{112,96},{1... | collective-permute-start | bytes 786440 | tf_op jit(solution)/shard_map/ppermute | solution.py:353
  6.0 1.0 %copy-start.1 = (f32[8,16,512]{2,1,0:T(8,128)S(1)}, f32[8,16,512]{2,1,0:T(8,128)}, u32[]{:S(2)}) copy-start(f32[8,16,512]{2,1,0:T(8,128)} %field_ref.1) | copy-start | bytes 786436
  12.0 8.7 %collective-permute-start.2 = (f32[14,8,512]{2,1,0:T(8,128)S(1)}, f32[14,8,512]{2,1,0:T(8,128)S(1)}, u32[]{:S(2)}, u32[]{:S(2)}) collective-permute-start(f32[14,8,512]{2,1,0:T(8,128)S(1)} %get-tuple-element.19), channel_id=1, source_target_pairs={{1,2},{2,1},{3,4},{4,3},{5,6},{6,5},{7,8},{8,7},{9,10},{10,9},{11,... | collective-permute-start | bytes 688136 | tf_op jit(solution)/shard_map/ppermute | solution.py:353
  17.0 3.7 %collective-permute-start.3 = (f32[14,8,512]{2,1,0:T(8,128)S(1)}, f32[14,8,512]{2,1,0:T(8,128)S(1)}, u32[]{:S(2)}, u32[]{:S(2)}) collective-permute-start(f32[14,8,512]{2,1,0:T(8,128)S(1)} %get-tuple-element.20), channel_id=1, source_target_pairs={{0,1},{1,0},{2,3},{3,2},{4,5},{5,4},{6,7},{7,6},{8,9},{9,8},{10,11... | collective-permute-start | bytes 688136 | tf_op jit(solution)/shard_map/ppermute | solution.py:353

commit v8 on v7

--- a/solution.py
+++ b/solution.py
@@ -260,11 +260,11 @@
         yield 2 * n + 1, planes - 1 - HX + d, planes - 1 - HX + other, rows
 
 
-def pack_rows(u_ref, out_ref, high):
+def pack_rows(u_ref, out_ref, high, base):
     planes, rows, bz = u_ref.shape
-    bx = planes - 2 * HX
     start = pl.multiple_of(jnp.where(high, rows - 2 * HY, HY), HY)
-    out_ref[0:bx] = u_ref[HX:HX + bx, pl.ds(start, HY)]
+    if base:
+        out_ref[0:base] = u_ref[HX:HX + base, pl.ds(start, HY)]
     row, _ = iotas()
     depth = jnp.where(high, HY - 1 - row, row)
     for n, x, y, count in shared_planes(planes):
@@ -272,21 +272,27 @@
             cols = slice(LANES * c, LANES * c + LANES)
             a, b = (u_ref[p, pl.ds(start, HY), cols] for p in (x, y))
             b = jnp.where(high, pltpu.roll(b, HY - count, 0), pltpu.roll(b, count, 0))
-            out_ref[bx + n, :, cols] = jnp.where(depth < count, a, b)
-
-
-def unpack_rows(in_ref, u_ref, high):
+            out_ref[base + n, :, cols] = jnp.where(depth < count, a, b)
+
+
+def unpack_rows(in_ref, u_ref, high, base):
     planes, rows, bz = u_ref.shape
-    bx = planes - 2 * HX
     start = pl.multiple_of(jnp.where(high, rows - HY, 0), HY)
-    u_ref[HX:HX + bx, pl.ds(start, HY)] = in_ref[0:bx]
+    if base:
+        u_ref[HX:HX + base, pl.ds(start, HY)] = in_ref[0:base]
     for n, x, y, count in shared_planes(planes):
         for c in range(bz // LANES):
             cols = slice(LANES * c, LANES * c + LANES)
-            both = in_ref[bx + n, :, cols]
+            both = in_ref[base + n, :, cols]
             u_ref[x, pl.ds(start, HY), cols] = both
             other = jnp.where(high, pltpu.roll(both, HY - count, 0), pltpu.roll(both, count, 0))
             u_ref[y, pl.ds(start, HY), cols] = other
+
+
+def edge_kernel(field_ref, rows_ref):
+    by = field_ref.shape[1]
+    start = pl.multiple_of(parity("py") * (by - HY), HY)
+    rows_ref[...] = field_ref[:, pl.ds(start, HY)]
 
 
 def place_kernel(own_ref, u_ref):
@@ -299,22 +305,23 @@
             u_ref[x:x + 1, y:y + HY] = edge
 
 
-def join_kernel(mid_ref, second_ref, first_ref, u_ref, first_out, second_out):
+def join_kernel(mid_ref, first_ref, second_ref, rows_ref, u_ref, first_out, second_out):
     bx, by, bz = first_ref.shape
     mine = slice(HY, HY + by)
     odd = parity("px")
     u_ref[pl.ds((1 - odd) * (HX + bx), HX), mine] = first_ref[pl.ds(odd * (bx - HX), HX)]
     u_ref[pl.ds(odd * (HX + bx), HX), mine] = second_ref[pl.ds((1 - odd) * (bx - HX), HX)]
     odd = parity("py")
-    pack_rows(u_ref, first_out, odd == 0)
-    pack_rows(u_ref, second_out, odd == 1)
-
-
-def first_kernel(mid_ref, second_ref, first_ref, gap_ref, dist_ref, u_ref, w0, w1, w2, sums_ref, q_ref):
+    u_ref[HX:HX + bx, pl.ds(pl.multiple_of(odd * (HY + by), HY), HY)] = rows_ref[...]
+    pack_rows(u_ref, first_out, odd == 0, bx)
+    pack_rows(u_ref, second_out, odd == 1, 0)
+
+
+def first_kernel(mid_ref, first_ref, second_ref, gap_ref, dist_ref, u_ref, w0, w1, w2, sums_ref, q_ref):
     planes = u_ref.shape[0]
     odd = parity("py")
-    unpack_rows(first_ref, u_ref, odd == 0)
-    unpack_rows(second_ref, u_ref, odd == 1)
+    unpack_rows(first_ref, u_ref, odd == 0, planes - 2 * HX)
+    unpack_rows(second_ref, u_ref, odd == 1, 0)
     krylov(u_ref, (w0, w1, w2), q_ref, 1, planes - 1, None, (gap_ref, dist_ref), sums_ref)
 
 
@@ -377,18 +384,20 @@
     own, whole = shape(bx, by, bz), shape(planes, rows, bz)
     sums = shape(devices, LANES)
     room = pltpu.VMEM(whole.shape, F32)
+    first = swap(start_field, "px", 0)
     second = swap(start_field, "px", 1)
-    first = swap(start_field, "px", 0)
-    strip = shape(bx + 2 * len(SHARED), HY, bz)
+    (rows_out,) = call(edge_kernel, "edge", (shape(bx, HY, bz),), start_field)
+    rows_in = swap(rows_out, "py", 1)
+    side, strip = shape(bx + 2 * len(SHARED), HY, bz), shape(2 * len(SHARED), HY, bz)
     (u,) = call(place_kernel, "place", (whole,), start_field)
-    u, first, second = call(join_kernel, "join", (whole, strip, strip), u, second, first, alias={0: 0})
+    u, first, second = call(join_kernel, "join", (whole, side, strip), u, first, second, rows_in, alias={0: 0})
+    first = swap(first, "py", 0)
     second = swap(second, "py", 1)
-    first = swap(first, "py", 0)
     parts = (shape(*known.shape), shape(*known.shape), shape(KNOWN, 8, LANES))
     known, gap, dist = call(gap_kernel, "gap", parts, start_field, known)
     step = (whole,) * 4 + (sums,)
     u, a0, a1, a2, sent = call(
-        first_kernel, "first_step", step, u, second, first, gap, dist, scratch=[room], alias={0: 0}
+        first_kernel, "first_step", step, u, first, second, gap, dist, scratch=[room], alias={0: 0}
     )
     recv = total_over_devices(sent)
     body = lambda *refs: second_kernel(cells, *refs)

time: 75.6 us -> 75 us (level)
  waiting for transfers between devices: 8.04 us -> 4.43 us
  starting transfers between devices: 10.4 us -> 13.9 us
    ppermute x4 -> x5, waiting for transfers between devices: 8.04 us -> 4.43 us  [swap(): return lax.ppermute(part, axis, pairs)]
    ppermute x4 -> x5, starting transfers between devices: 10.4 us -> 13.9 us  [swap(): return lax.ppermute(part, axis, pairs)]
    pallas_call x6 -> x7, Pallas kernels: 7.51 us -> 7.5 us  [call(): pl.pallas_call(body, out_shape=outs, in_specs=[vmem] * len(args), out_spe...]
  transfers between devices with their start and end apart: 4 -> 5, of which waited for: 2 -> 2; matrix products, arithmetic and copies ran while one was open for 0% -> 0% of each run, Pallas kernels for 1% -> 1%
where the time goes in v8:
time: 75 us; the launch traced here: 74.8 us
  blocking collectives  47.2 us (63%)
  starting transfers between devices  13.9 us (19%)
  Pallas kernels  7.5 us (10%)
  waiting for transfers between devices  4.43 us (6%)
  local copies, waits for them, and re-layouts  0.99 us (1%)
    all_to_all x2, blocking collectives, total_over_devices(): return lax.all_to_all(rows, AXES, 0, 0).reshape(count, LANES)  47.2 us
    ppermute x5, starting transfers between devices, swap(): return lax.ppermute(part, axis, pairs)  13.9 us
    pallas_call x7, Pallas kernels, call(): pl.pallas_call(body, out_shape=outs, in_specs=[vmem] * len(args), out_spe...  7.5 us
    ppermute x5, waiting for transfers between devices, swap(): return lax.ppermute(part, axis, pairs)  4.43 us
  transfers between devices with their start and end apart: 5, of which 2 were waited for; matrix products, arithmetic and copies ran while one was open for 0% of the time, Pallas kernels for 1%

profile of v8, /device:TPU:1, one launch (start us, length us, event | category | flops | bytes accessed | tf_op | source)
XLA Modules:
  0.0 74.8 jit_solution(10850580868633133168)
XLA Ops:
  0.6 0.7 collective-permute-start.1
  1.3 4.6 %collective-permute-start = (f32[8,16,512]{2,1,0:T(8,128)}, f32[8,16,512]{2,1,0:T(8,128)S(1)}, u32[]{:S(2)}, u32[]{:S(2)}) collective-permute-start(f32[8,16,512]{2,1,0:T(8,128)} %field_ref.3), channel_id=1, source_target_pairs={{0,16},{16,0},{32,48},{48,32},{64,80},{80,64},{96,112},{112,96},{1... | collective-permute-start | bytes 786440 | tf_op jit(solution)/shard_map/ppermute | solution.py:360
  5.9 0.0 copy-start
  5.9 1.0 %copy-done = f32[8,16,512]{2,1,0:T(8,128)S(1)} copy-done((f32[8,16,512]{2,1,0:T(8,128)S(1)}, f32[8,16,512]{2,1,0:T(8,128)}, u32[]{:S(2)}) %copy-start) | copy-done | bytes 262168
  6.9 4.7 %collective-permute-start.2 = (f32[8,8,512]{2,1,0:T(8,128)S(1)}, f32[8,8,512]{2,1,0:T(8,128)S(1)}, u32[]{:S(2)}, u32[]{:S(2)}) collective-permute-start(f32[8,8,512]{2,1,0:T(8,128)S(1)} %edge.1), channel_id=1, source_target_pairs={{1,2},{2,1},{3,4},{4,3},{5,6},{6,5},{7,8},{8,7},{9,10},{10,9},{11,... | collective-permute-start | bytes 393224 | tf_op jit(solution)/shard_map/ppermute | solution.py:360
  11.6 0.0 copy-start.1
  11.6 2.6 %collective-permute-done.2.rows_ref = f32[8,8,512]{2,1,0:T(8,128)S(1)} collective-permute-done((f32[8,8,512]{2,1,0:T(8,128)S(1)}, f32[8,8,512]{2,1,0:T(8,128)S(1)}, u32[]{:S(2)}, u32[]{:S(2)}) %collective-permute-start.2) | collective-permute-done | bytes 131104 | tf_op jit(solution)/shard_map/ppermute | solution.py:360
  14.2 0.0 collective-permute-done.1.second_ref
  14.2 0.0 collective-permute-done.first_ref
  14.2 0.1 join.1
  14.3 0.1 collective-permute-start.3
  14.4 3.9 %collective-permute-start.4 = (f32[6,8,512]{2,1,0:T(8,128)S(1)}, f32[6,8,512]{2,1,0:T(8,128)S(1)}, u32[]{:S(2)}, u32[]{:S(2)}) collective-permute-start(f32[6,8,512]{2,1,0:T(8,128)S(1)} %get-tuple-element.20), channel_id=1, source_target_pairs={{1,2},{2,1},{3,4},{4,3},{5,6},{6,5},{7,8},{8,7},{9,10},{10,9},{11,... | collective-permute-start | bytes 294920 | tf_op jit(solution)/shard_map/ppermute | solution.py:360
  18.3 0.0 copy-done.1
  18.3 0.4 gap.1
  18.8 1.8 %collective-permute-done.4.second_ref = f32[6,8,512]{2,1,0:T(8,128)S(1)} collective-permute-done((f32[6,8,512]{2,1,0:T(8,128)S(1)}, f32[6,8,512]{2,1,0:T(8,128)S(1)}, u32[]{:S(2)}, u32[]{:S(2)}) %collective-permute-start.4) | collective-permute-done | bytes 98336 | tf_op jit(solution)/shard_map/ppermute | solution.py:360
  20.6 0.0 collective-permute-done.3.first_ref
  20.6 2.8 %first_step.1 = (f32[22,32,512]{2,1,0:T(8,128)S(1)}, f32[22,32,512]{2,1,0:T(8,128)S(1)}, f32[22,32,512]{2,1,0:T(8,128)S(1)}, f32[22,32,512]{2,1,0:T(8,128)S(1)}, f32[256,128]{1,0:T(8,128)S(1)}) custom-call(f32[22,32,512]{2,1,0:T(8,128)S(1)} %get-tuple-element.18.mid_ref, ...), custom_call_target="tpu_custom_call", output_to_operand_aliasing={{0}: (0, {})} | custom-call | tf_op jit(solution)/shard_map/first_step/pallas_call | solution.py:372
  23.4 28.6 %all_to_all.10 = f32[256,1,128]{2,1,0:T(1,128)S(1)} all-to-all(f32[256,1,128]{2,1,0:T(1,128)S(1)} %bitcast.11), channel_id=1, replica_groups=mesh['px'=16,'py'=16] {'px','py'}, dimensions={0} | all-to-all | bytes 262144 | tf_op jit(solution)/shard_map/all_to_all | solution.py:353
  52.0 2.8 %second_step.1 = (f32[22,32,512]{2,1,0:T(8,128)S(1)}, f32[22,32,512]{2,1,0:T(8,128)S(1)}, f32[22,32,512]{2,1,0:T(8,128)S(1)}, f32[22,32,512]{2,1,0:T(8,128)S(1)}, f32[256,128]{1,0:T(8,128)S(1)}) custom-call(f32[256,128]{1,0:T(8,128)S(1)} %bitcast.8, f32[22,32,512]{2,1,0:T(8,128)S(1)} %get-tuple-element.24.refs_1_, ...), custom_call_target="tpu_custom_call" | custom-call | tf_op jit(solution)/shard_map/second_step/pallas_call | solution.py:372
  54.9 18.6 %all_to_all.11 = f32[256,1,128]{2,1,0:T(1,128)S(1)} all-to-all(f32[256,1,128]{2,1,0:T(1,128)S(1)} %bitcast.10), channel_id=1, replica_groups=mesh['px'=16,'py'=16] {'px','py'}, dimensions={0} | all-to-all | bytes 262144 | tf_op jit(solution)/shard_map/all_to_all | solution.py:353
  73.5 1.3 %finish.1 = (f32[8,16,512]{2,1,0:T(8,128)}, f32[8,16,512]{2,1,0:T(8,128)}) custom-call(f32[256,128]{1,0:T(8,128)S(1)} %bitcast.9, f32[22,32,512]{2,1,0:T(8,128)S(1)} %get-tuple-element.30.refs_1_, f32[22,32,512]{2,1,0:T(8,128)S(1)} %get-tuple-element.31.refs_2_, f32[22,32,512]{2,1,0:T(8,128)S(1)} %get-tuple-element.32.refs_3_, ...), custom_call_target="tpu_custom_call" | custom-call | tf_op jit(solution)/shard_map/finish/pallas_call | solution.py:372
  (2 shorter events, 0.0 us)
Async XLA Ops:
  0.6 13.6 %collective-permute-start.1 = (f32[8,16,512]{2,1,0:T(8,128)}, f32[8,16,512]{2,1,0:T(8,128)S(1)}, u32[]{:S(2)}, u32[]{:S(2)}) collective-permute-start(f32[8,16,512]{2,1,0:T(8,128)} %field_ref.3), channel_id=1, source_target_pairs={{16,32},{32,16},{48,64},{64,48},{80,96},{96,80},{112,128},{128,112... | collective-permute-start | bytes 786440 | tf_op jit(solution)/shard_map/ppermute | solution.py:360
  1.3 12.9 %collective-permute-start = (f32[8,16,512]{2,1,0:T(8,128)}, f32[8,16,512]{2,1,0:T(8,128)S(1)}, u32[]{:S(2)}, u32[]{:S(2)}) collective-permute-start(f32[8,16,512]{2,1,0:T(8,128)} %field_ref.3), channel_id=1, source_target_pairs={{0,16},{16,0},{32,48},{48,32},{64,80},{80,64},{96,112},{112,96},{1... | collective-permute-start | bytes 786440 | tf_op jit(solution)/shard_map/ppermute | solution.py:360
  5.9 1.0 %copy-start = (f32[8,16,512]{2,1,0:T(8,128)S(1)}, f32[8,16,512]{2,1,0:T(8,128)}, u32[]{:S(2)}) copy-start(f32[8,16,512]{2,1,0:T(8,128)} %field_ref.3) | copy-start | bytes 786436
  6.9 7.3 %collective-permute-start.2 = (f32[8,8,512]{2,1,0:T(8,128)S(1)}, f32[8,8,512]{2,1,0:T(8,128)S(1)}, u32[]{:S(2)}, u32[]{:S(2)}) collective-permute-start(f32[8,8,512]{2,1,0:T(8,128)S(1)} %edge.1), channel_id=1, source_target_pairs={{1,2},{2,1},{3,4},{4,3},{5,6},{6,5},{7,8},{8,7},{9,10},{10,9},{11,... | collective-permute-start | bytes 393224 | tf_op jit(solution)/shard_map/ppermute | solution.py:360
  11.6 6.7 %copy-start.1 = (f32[8,8,16,512]{3,2,1,0:T(8,128)S(1)}, f32[8,8,16,512]{3,2,1,0:T(8,128)}, u32[]{:S(2)}) copy-start(f32[8,8,16,512]{3,2,1,0:T(8,128)} %known_ref.1) | copy-start | bytes 6291460
  14.3 6.3 %collective-permute-start.3 = (f32[14,8,512]{2,1,0:T(8,128)S(1)}, f32[14,8,512]{2,1,0:T(8,128)S(1)}, u32[]{:S(2)}, u32[]{:S(2)}) collective-permute-start(f32[14,8,512]{2,1,0:T(8,128)S(1)} %get-tuple-element.19), channel_id=1, source_target_pairs={{0,1},{1,0},{2,3},{3,2},{4,5},{5,4},{6,7},{7,6},{8,9},{9,8},{10,11... | collective-permute-start | bytes 688136 | tf_op jit(solution)/shard_map/ppermute | solution.py:360
  14.4 6.2 %collective-permute-start.4 = (f32[6,8,512]{2,1,0:T(8,128)S(1)}, f32[6,8,512]{2,1,0:T(8,128)S(1)}, u32[]{:S(2)}, u32[]{:S(2)}) collective-permute-start(f32[6,8,512]{2,1,0:T(8,128)S(1)} %get-tuple-element.20), channel_id=1, source_target_pairs={{1,2},{2,1},{3,4},{4,3},{5,6},{6,5},{7,8},{8,7},{9,10},{10,9},{11,... | collective-permute-start | bytes 294920 | tf_op jit(solution)/shard_map/ppermute | solution.py:360
